TPU v7x, 32 devices: a whole 2x2x4 slice. The times are simulated.
32 devices in a mesh: src: 4 (over y, x), snk: 4 (over z), slab: 2 (over core).
Axes of the slice: x: 2, y: 2, z: 4, core: 2. Of those that a mesh axis runs over, the one named last changes fastest.
Arguments:
- eigvecs: bfloat16 [8, 8192, 384], P('snk', ('src', 'slab')), may hold values from -0.125 to 0.125
- perambulator: bfloat16 [8, 8, 4, 192, 384], P('snk', 'src'), may hold values from -0.4375 to 0.4375
- momenta: int32 [4, 3], replicated, may hold values from 1 to 3
- source_times: int32 [8], P('src'), may hold values from 0 to 7, as said below
Outputs:
- blocks: float32 [4, 8, 8, 4, 192, 384], P(None, 'snk', 'src', None, 'slab')
Inputs may be any that keep to these rules, and one draw needn't show every extreme that they name: `source_times`: distinct time slices.
All inputs are finite; a program needn't handle non-finite values.
Results may differ from a plain program's by a relative error of at most 0.0062.
Values may be sent and summed in bfloat16 or wider, within the bound.
No kernel may reach another device: no remote copies, remote signals or barrier semaphores. Data moves between devices by JAX's collectives and lax.ppermute only.
A program may use at most 128 MiB of HBM per device.

v0:
```python
import math

import jax
import jax.numpy as jnp
from jax import lax
from jax.sharding import PartitionSpec as P

LX = 32
LY = 32
ZPL = 1


def angles(momenta, xs, ys, zs, lz):
    fx = (momenta[:, 0:1] * xs[None, :] % LX).astype(jnp.float32) / LX
    fy = (momenta[:, 1:2] * ys[None, :] % LY).astype(jnp.float32) / LY
    fz = (momenta[:, 2:3] * zs[None, :] % lz).astype(jnp.float32) / lz
    return 2.0 * math.pi * (fx + fy + fz)


def local(eigvecs, perambulator, momenta, source_times):
    nev = eigvecs.shape[2] // 2
    count = eigvecs.shape[1]
    slabs = lax.axis_size("slab")
    lz = ZPL * lax.axis_size("src") * slabs
    sites = jnp.arange(count, dtype=jnp.int32)
    xs = sites % LX
    ys = sites // LX % LY
    zs = sites // (LX * LY) + lax.axis_index(("src", "slab")) * ZPL
    angle = angles(momenta, xs, ys, zs, lz)
    vreal = eigvecs[:, :, :nev].astype(jnp.float32)
    vimag = eigvecs[:, :, nev:].astype(jnp.float32)
    partials = []
    for m in range(angle.shape[0]):
        cosine = jnp.cos(angle[m])[None, :, None]
        sine = jnp.sin(angle[m])[None, :, None]
        phased = jnp.concatenate(
            [cosine * vreal + sine * vimag, cosine * vimag - sine * vreal], axis=2
        ).astype(jnp.bfloat16)
        gram = jnp.einsum("tsa,tsb->tab", eigvecs, phased, preferred_element_type=jnp.float32)
        real = gram[:, :nev, :nev] + gram[:, nev:, nev:]
        imag = gram[:, :nev, nev:] - gram[:, nev:, :nev]
        partials.append(jnp.concatenate([real, imag], axis=2))
    partial_value = jnp.stack(partials, axis=1)
    tdev = partial_value.shape[0]
    rows = nev // slabs
    local_times = lax.axis_index("snk") * tdev + jnp.arange(tdev, dtype=jnp.int32)
    slab_part = lax.psum_scatter(partial_value, "slab", scatter_dimension=2, tiled=True)
    share = lax.psum_scatter(slab_part, "src", scatter_dimension=2, tiled=True).astype(jnp.bfloat16)
    sink = lax.all_gather(share, "src", axis=2, tiled=True)
    selector = (source_times[:, None] == local_times[None, :]).astype(jnp.bfloat16)
    term = jnp.dot(selector, sink.reshape(tdev, -1), preferred_element_type=jnp.float32)
    picked = lax.psum(term.astype(jnp.bfloat16), "snk")
    picked = picked.reshape((source_times.shape[0],) + sink.shape[1:])
    source = lax.all_gather(picked, "slab", axis=2, tiled=True)
    stacked = jnp.concatenate([sink[..., :nev], sink[..., nev:]], axis=2)
    prod = jnp.einsum(
        "tmra,tsqab->mtsqrb", stacked, perambulator, preferred_element_type=jnp.float32
    )
    creal = prod[..., :rows, :nev] - prod[..., rows:, nev:]
    cimag = prod[..., :rows, nev:] + prod[..., rows:, :nev]
    half = jnp.concatenate([creal, cimag], axis=4).astype(jnp.bfloat16)
    both = jnp.concatenate([source[..., :nev], source[..., nev:]], axis=2)
    quad = jnp.einsum("mtsqrb,smcb->mtsqrc", half, both, preferred_element_type=jnp.float32)
    dreal = quad[..., :rows, :nev] + quad[..., rows:, nev:]
    dimag = quad[..., rows:, :nev] - quad[..., :rows, nev:]
    return jnp.concatenate([dreal, dimag], axis=-1)


def solution(mesh):
    placed = (P("snk", ("src", "slab"), None), P("snk", "src", None, None, None), P(), P("src"))
    return jax.shard_map(
        local,
        mesh=mesh,
        in_specs=placed,
        out_specs=P(None, "snk", "src", None, "slab", None),
        check_vma=False,
    )
```

profile of v0, /device:TPU:0, one launch (start us, length us, event | category | flops | bytes accessed | tf_op | source)
XLA Modules:
  0.0 186.2 jit_solution(4424322251207634354)
XLA Ops:
  6.5 1.1 slice_reduce_fusion.2
  8.3 2.6 %fusion.9 = (bf16[2,1024,192]{2,1,0:T(8,128)(2,1)S(1)}, bf16[2,1024,192]{2,1,0:T(8,128)(2,1)S(1)}) fusion(f32[1024]{0:T(1024)S(1)} %bitcast.63, f32[1024]{0:T(1024)S(1)} %bitcast.64, bf16[2,1024,384]{2,1,0:T(8,128)(2,1)} %param.4), kind=kLoop, calls=%fused_computation.35 | loop fusion | flops 3932160 | bytes 3153920 | tf_op jit(solution)/shard_map/convert.6
  10.9 1.2 fusion.42
  12.4 3.0 %fusion.5 = (bf16[2,1024,192]{2,1,0:T(8,128)(2,1)S(1)}, bf16[2,1024,192]{2,1,0:T(8,128)(2,1)S(1)}, bf16[2,1024,192]{2,1,0:T(8,128)(2,1)S(1)}, bf16[2,1024,192]{2...) fusion(f32[1024]{0:T(1024)S(1)} %bitcast.58, f32[1024]{0:T(1024)S(1)} %bitcast.57, ...), kind=kLoop, calls=%fused_computation.31 | loop fusion | flops 10223616 | bytes 6316032 | tf_op jit(solution)/shard_map/convert.8
  15.3 1.2 fusion.45
  16.8 1.2 fusion.39
  18.2 1.2 fusion.36
  20.4 1.6 pad_maximum_fusion.2
  22.0 12.9 %reduce-scatter.3.cloned.1.call-done = f32[2,4,96,384]{3,2,0,1:T(8,128)} async-done(((f32[2,4,192,384]{3,2,0,1:T(8,128)}), f32[2,4,96,384]{3,2,0,1:T(8,128)}) %reduce-scatter.3.cloned.1.call-update) | async-done | bytes 1179664 | tf_op jit(solution)/shard_map/reduce_scatter | solution.py:47
  35.0 32.9 %reduce-scatter.5.cloned.1.call-done = f32[2,4,24,384]{3,2,0,1:T(8,128)} async-done(((f32[2,4,96,384]{3,2,0,1:T(8,128)}), f32[2,4,24,384]{3,2,0,1:T(8,128)}) %reduce-scatter.5.cloned.1.call-update) | async-done | bytes 294928 | tf_op jit(solution)/shard_map/reduce_scatter | solution.py:48
  67.9 1.0 convert_element_type.32
  68.8 10.6 %all_gather.6 = bf16[2,4,96,384]{3,2,0,1:T(8,128)(2,1)S(1)} all-gather(bf16[2,4,24,384]{3,2,0,1:T(8,128)(2,1)S(1)} %convert_element_type.32), channel_id=1, replica_groups=mesh['src'=4,'snk'=4,'slab'=2] {'src'}, dimensions={2}, use_global_device_ids=true | all-gather | bytes 737280 | tf_op jit(solution)/shard_map/all_gather | solution.py:49
  80.1 0.8 convolution_convert_fusion
  81.1 1.1 copy.27
  82.4 1.0 fusion.80
  83.4 38.6 %all-reduce.2.cloned.1.call-done = bf16[2,4,96,384]{3,1,0,2:T(4,128)(2,1)} async-done(((bf16[2,4,96,384]{3,1,0,2:T(4,128)(2,1)}), bf16[2,4,96,384]{3,1,0,2:T(4,128)(2,1)}) %all-reduce.2.cloned.1.call-update) | async-done | bytes 589840 | tf_op jit(solution)/shard_map/psum | solution.py:52
  122.1 3.6 %convolution_bitcast_fusion = f32[4,2,2,4,192,384]{5,4,3,2,0,1:T(8,128)S(1)} fusion(bf16[2,2,4,192,384]{4,3,2,1,0:T(8,128)(2,1)S(1)} %copy-done, bf16[2,4,96,192]{3,2,0,1:T(8,128)(2,1)} %get-tuple-element.35, bf16[2,4,96,192]{3,2,0,1:T(8,128)(2,1)S(1)} %get-tuple-element.34), kind=kOutput, calls=%fused_computation.2 | convolution fusion | flops 1813118976 | bytes 21823488 | tf_op jit(solution)/shard_map/tmra,tsqab->mtsqrb/dot_general | solution.py:56
  125.7 5.7 %fusion.1 = (bf16[4,2,2,4,96,192]{5,4,3,2,0,1:T(8,128)(2,1)}, bf16[4,2,2,4,96,192]{5,4,3,2,0,1:T(8,128)(2,1)}) fusion(f32[4,2,2,4,192,384]{5,4,3,2,0,1:T(8,128)S(1)} %convolution_bitcast_fusion), kind=kLoop, calls=%fused_computation.9 | loop fusion | flops 4718592 | bytes 23592960 | tf_op jit(solution)/shard_map/convert
  131.3 0.8 all-gather.2.cloned.1.call-done
  132.1 2.2 %fusion.79 = (bf16[2,4,192,192]{3,1,0,2:T(4,128)(2,1)S(1)}, bf16[2,4,192,192]{3,1,0,2:T(4,128)(2,1)S(1)}) fusion(bf16[2,4,192,384]{3,1,0,2:T(4,128)(2,1)} %all-gather.2.cloned.1.call-done), kind=kLoop, calls=%fused_computation.149 | loop fusion | bytes 2359296 | tf_op jit(solution)/shard_map/slice | solution.py:62
  135.7 10.2 %convolution_bitcast_fusion.1 = f32[4,2,2,4,192,384]{5,4,3,1,2,0:T(8,128)} fusion(bf16[2,4,192,192]{2,3,0,1:T(8,128)(2,1)S(1)} %copy.43, bf16[2,4,192,192]{2,3,0,1:T(8,128)(2,1)S(1)} %copy.42, bf16[4,2,2,4,96,192]{5,4,3,2,0,1:T(8,128)(2,1)} %get-tuple-element.11, bf16[4,2,2,4,96,192]{5,4,3,2,0,1:T(8,128)(2,1)} %get-tuple-element.10), kind=kOutput, calls=%fused_computation.3 | convolution fusion | flops 1823735808 | bytes 24772608 | tf_op jit(solution)/shard_map/mtsqrb,smcb->mtsqrc/dot_general | solution.py:63
  145.9 15.1 %slice_add_fusion = (f32[4,2,2,4,96,192]{5,4,3,1,2,0:T(8,128)}, f32[4,2,2,4,96,192]{5,4,3,1,2,0:T(8,128)}) fusion(f32[4,2,2,4,192,384]{5,4,3,1,2,0:T(8,128)} %convolution_bitcast_fusion.1), kind=kLoop, calls=%fused_computation.5 | loop fusion | flops 2359296 | bytes 28311552 | tf_op jit(solution)/shard_map/add | solution.py:64
  161.0 10.3 %pad_maximum_fusion = f32[4,2,2,4,96,384]{5,4,3,1,2,0:T(8,128)} fusion(f32[4,2,2,4,96,192]{5,4,3,1,2,0:T(8,128)} %get-tuple-element.9, f32[4,2,2,4,96,192]{5,4,3,1,2,0:T(8,128)} %get-tuple-element.8), kind=kLoop, calls=%fused_computation.1 | loop fusion | flops 2359296 | bytes 18874368 | tf_op jit(solution)/shard_map/concatenate | solution.py:66
  171.3 8.4 %copy.32 = f32[4,2,2,4,96,384]{5,4,3,2,1,0:T(8,128)} copy(f32[4,2,2,4,96,384]{5,4,3,1,2,0:T(8,128)} %pad_maximum_fusion) | data formatting | bytes 18874368 | tf_op jit(solution)/shard_map/concatenate | solution.py:66
  (34 shorter events, 4.9 us)
Async XLA Ops:
  6.5 115.5 %copy-start = (bf16[2,2,4,192,384]{4,3,2,1,0:T(8,128)(2,1)S(1)}, bf16[2,2,4,192,384]{4,3,2,1,0:T(8,128)(2,1)}, u32[]{:S(2)}) copy-start(bf16[2,2,4,192,384]{4,3,2,1,0:T(8,128)(2,1)} %param.5) | copy-start | bytes 7077892
  6.5 28.4 %reduce-scatter.3.cloned.1.call-start = ((), (), s32[]{:S(2)}) async-start(), calls=%async_computation.2 | async-start | bytes 3538944 | tf_op jit(solution)/shard_map/reduce_scatter | solution.py:47
  8.2 2.6 %copy-start.2 = (bf16[2,1024,384]{2,1,0:T(8,128)(2,1)S(1)}, bf16[2,1024,384]{2,1,0:T(8,128)(2,1)}, u32[]{:S(2)}) copy-start(bf16[2,1024,384]{2,1,0:T(8,128)(2,1)} %param.4) | copy-start | bytes 4718596
  21.9 45.9 %reduce-scatter.5.cloned.1.call-start = ((), (), s32[]{:S(2)}) async-start(), calls=%async_computation.3 | async-start | bytes 1474560 | tf_op jit(solution)/shard_map/reduce_scatter | solution.py:48
  34.9 45.2 %copy-start.3 = (s32[2]{0:T(128)S(1)}, s32[2]{0:T(128)}, u32[]{:S(2)}) copy-start(s32[2]{0:T(128)} %param.7) | copy-start | bytes 28
  35.0 87.1 %all-reduce.2.cloned.1.call-start = ((), (), s32[]{:S(2)}) async-start(), calls=%async_computation.4 | async-start | bytes 1179648 | tf_op jit(solution)/shard_map/psum | solution.py:52
  82.2 49.9 %all-gather.2.cloned.1.call-start = ((), (), s32[]{:S(2)}) async-start(), calls=%async_computation.5 | async-start | bytes 1769472 | tf_op jit(solution)/shard_map/all_gather | solution.py:54
  171.3 8.4 %copy-start.1 = (bf16[2,2,4,192,384]{4,3,2,1,0:T(8,128)(2,1)S(1)}, bf16[2,2,4,192,384]{4,3,2,1,0:T(8,128)(2,1)}, u32[]{:S(2)}) copy-start(bf16[2,2,4,192,384]{4,3,2,1,0:T(8,128)(2,1)} %param.5) | copy-start | bytes 7077892
Sparse Core Ops, SparseCore 0:
  22.1 12.8 reduce-scatter.2
  37.8 29.9 reduce-scatter.4
  82.3 39.6 all-reduce.1
  123.4 8.6 all-gather.1
where the time goes:
time: 186 us
  waiting for transfers between devices  85.3 us (46%)
  other arithmetic  41.1 us (22%)
  matrix products  19.4 us (10%)
  local copies, waits for them, and re-layouts  16.3 us (9%)
  between operations  13.3 us (7%)
  blocking collectives  10.6 us (6%)
    psum x1, waiting for transfers between devices, local(): picked = lax.psum(term.astype(jnp.bfloat16), 'snk')  38.6 us
    reduce_scatter x1, waiting for transfers between devices, local(): lax.psum_scatter(slab_part, 'src', scatter_dimension=2, tiled=True)  32.9 us
    add x1, other arithmetic, local(): dreal = quad[..., :rows, :nev] + quad[..., rows:, nev:]  15.1 us
    reduce_scatter x1, waiting for transfers between devices, local(): lax.psum_scatter(partial_value, 'slab', scatter_dimension=2, tiled=True)  12.9 us
    another operation x3, other arithmetic  11.2 us
    all_gather x1, blocking collectives, local(): sink = lax.all_gather(share, 'src', axis=2, tiled=True)  10.6 us
    concatenate x1, other arithmetic, local(): return jnp.concatenate([dreal, dimag], axis=-1)  10.3 us
    dot_general x1, matrix products, local(): jnp.einsum('mtsqrb,smcb->mtsqrc', half, both, preferred_element_type=jnp....  10.2 us
  transfers between devices with their start and end apart: 4, of which 4 were waited for; matrix products, arithmetic and copies ran while one was open for 5% of the time, Pallas kernels for 0%

commit v1 on v0

v1 whole, which is shorter than its diff:
```python
import functools
import math

import jax
import jax.numpy as jnp
from jax import lax
from jax.experimental import pallas as pl
from jax.experimental.pallas import tpu as pltpu
from jax.sharding import PartitionSpec as P

LX = 32
LY = 32
TAIL = 16
F32 = jnp.float32
BF16 = jnp.bfloat16
VMEM = pl.BlockSpec(memory_space=pltpu.VMEM)
SMEM = pl.BlockSpec(memory_space=pltpu.SMEM)


def angles(momenta, xs, ys, zs, lz):
    fx = (momenta[:, 0:1] * xs[None, :] % LX).astype(F32) / LX
    fy = (momenta[:, 1:2] * ys[None, :] % LY).astype(F32) / LY
    fz = (momenta[:, 2:3] * zs[None, :] % lz).astype(F32) / lz
    return 2.0 * math.pi * (fx + fy + fz)


def general(eigvecs, perambulator, momenta, source_times):
    nev = eigvecs.shape[2] // 2
    count = eigvecs.shape[1]
    zpl = count // (LX * LY)
    slabs = lax.axis_size("slab")
    lz = zpl * lax.axis_size("src") * slabs
    sites = jnp.arange(count, dtype=jnp.int32)
    xs = sites % LX
    ys = sites // LX % LY
    zs = sites // (LX * LY) + lax.axis_index(("src", "slab")) * zpl
    angle = angles(momenta, xs, ys, zs, lz)
    vreal = eigvecs[:, :, :nev].astype(F32)
    vimag = eigvecs[:, :, nev:].astype(F32)
    partials = []
    for m in range(angle.shape[0]):
        cosine = jnp.cos(angle[m])[None, :, None]
        sine = jnp.sin(angle[m])[None, :, None]
        phased = jnp.concatenate(
            [cosine * vreal + sine * vimag, cosine * vimag - sine * vreal], axis=2
        ).astype(BF16)
        gram = jnp.einsum("tsa,tsb->tab", eigvecs, phased, preferred_element_type=F32)
        real = gram[:, :nev, :nev] + gram[:, nev:, nev:]
        imag = gram[:, :nev, nev:] - gram[:, nev:, :nev]
        partials.append(jnp.concatenate([real, imag], axis=2))
    partial_value = jnp.stack(partials, axis=1)
    tdev = partial_value.shape[0]
    rows = nev // slabs
    local_times = lax.axis_index("snk") * tdev + jnp.arange(tdev, dtype=jnp.int32)
    slab_part = lax.psum_scatter(partial_value, "slab", scatter_dimension=2, tiled=True)
    share = lax.psum_scatter(slab_part, "src", scatter_dimension=2, tiled=True).astype(BF16)
    sink = lax.all_gather(share, "src", axis=2, tiled=True)
    selector = (source_times[:, None] == local_times[None, :]).astype(BF16)
    term = jnp.dot(selector, sink.reshape(tdev, -1), preferred_element_type=F32)
    picked = lax.psum(term.astype(BF16), "snk")
    picked = picked.reshape((source_times.shape[0],) + sink.shape[1:])
    source = lax.all_gather(picked, "slab", axis=2, tiled=True)
    stacked = jnp.concatenate([sink[..., :nev], sink[..., nev:]], axis=2)
    prod = jnp.einsum("tmra,tsqab->mtsqrb", stacked, perambulator, preferred_element_type=F32)
    creal = prod[..., :rows, :nev] - prod[..., rows:, nev:]
    cimag = prod[..., :rows, nev:] + prod[..., rows:, :nev]
    half = jnp.concatenate([creal, cimag], axis=4).astype(BF16)
    both = jnp.concatenate([source[..., :nev], source[..., nev:]], axis=2)
    quad = jnp.einsum("mtsqrb,smcb->mtsqrc", half, both, preferred_element_type=F32)
    dreal = quad[..., :rows, :nev] + quad[..., rows:, nev:]
    dimag = quad[..., rows:, :nev] - quad[..., :rows, nev:]
    return jnp.concatenate([dreal, dimag], axis=-1)


def turned(x, nev):
    return jnp.concatenate([x[:, nev:], -x[:, :nev]], axis=1)


def gram_kernel(nsrc, slabs, lz, sibling, mom_ref, eig_ref, *refs):
    if sibling:
        acc_in, times_ref = refs[:2]
        outs = refs[2 : 2 + nsrc]
        tab, turn, wide, tran, acc = refs[2 + nsrc :]
    else:
        (acc_out,) = refs[:1]
        tab, turn, wide, tran, acc = refs[1:]
    times, count, width = eig_ref.shape
    nev = width // 2
    rows = nev // slabs
    src = lax.axis_index("src")
    slab = lax.axis_index("slab")
    z = src * slabs + (1 - slab if sibling else slab)
    index = lax.broadcasted_iota(jnp.int32, (LX, 128), 0)
    for k in range(nsrc):
        m = src ^ k
        ax = (2.0 * math.pi) * ((mom_ref[m, 0] * index % LX).astype(F32) / LX)
        fz = (mom_ref[m, 2] * z % lz).astype(F32) / lz
        ay = (2.0 * math.pi) * ((mom_ref[m, 1] * index % LY).astype(F32) / LY + fz)
        tab[0, k] = jnp.cos(ax)
        tab[1, k] = jnp.sin(ax)
        tab[2, k] = jnp.cos(ay)
        tab[3, k] = jnp.sin(ay)
    wides = width // 128
    for t in range(times):
        tran[...] = eig_ref[t].T

        def phase(y, _):
            at = pl.multiple_of(y * LX, LX)
            v = eig_ref[t, pl.ds(at, LX), :].astype(F32)
            u = turned(v, nev)
            for k in range(nsrc):
                cy = jnp.broadcast_to(tab[2, k, pl.ds(y, 1), :], (LX, 128))
                sy = jnp.broadcast_to(tab[3, k, pl.ds(y, 1), :], (LX, 128))
                cx, sx = tab[0, k], tab[1, k]
                c = cx * cy - sx * sy
                s = sx * cy + cx * sy
                c = jnp.concatenate([c] * wides, axis=1)
                s = jnp.concatenate([s] * wides, axis=1)
                wide[pl.ds(at, LX), k * width : (k + 1) * width] = (c * v + s * u).astype(BF16)
            return 0

        lax.fori_loop(0, count // LX, phase, 0)
        at_r = pl.multiple_of(slab * rows, rows)
        at_i = pl.multiple_of(slab * rows + nev, rows)
        for k in range(nsrc):
            w = wide[:, k * width : (k + 1) * width]
            up = jnp.dot(tran[pl.ds(at_r, rows), :], w, preferred_element_type=F32)
            lo = jnp.dot(tran[pl.ds(at_i, rows), :], w, preferred_element_type=F32)
            e = up + turned(lo, nev)
            if sibling:
                e = e + acc_in[k, t]
                if k == 0:
                    outs[0][t] = e
                else:
                    outs[k][t, :rows, :] = e.astype(BF16)
                    outs[k][t, rows:, :] = jnp.full((TAIL, width), times_ref[t].astype(F32), F32).astype(BF16)
            else:
                acc_out[k, t] = e


def sum_kernel(own, *refs):
    out = refs[-1]
    rows = own.shape[1]
    total = own[...]
    for r in refs[:-1]:
        total = total + r[:, :rows, :].astype(F32)
    out[...] = total.astype(BF16)


def pick_kernel(nsnk, nsrc, times_ref, *refs):
    sent = refs[: nsrc - 1]
    seen = refs[nsrc - 1 : nsrc - 1 + nsnk]
    outs = refs[nsrc - 1 + nsnk :]
    tdev, rows, width = seen[0].shape
    snk = lax.axis_index("snk")
    for k in range(nsrc):
        for s in range(outs[k].shape[0]):
            if k == 0:
                want = jnp.full((TAIL, width), times_ref[s].astype(F32), F32)
            else:
                want = sent[k - 1][s, rows:, :].astype(F32)
            mask = []
            for d in range(nsnk):
                for t in range(tdev):
                    time = (lax.rem(snk + nsnk - d, nsnk) * tdev + t).astype(F32)
                    mask.append((want == time).astype(F32))
            for r in range(rows // TAIL):
                total = jnp.zeros((TAIL, width), F32)
                for d in range(nsnk):
                    for t in range(tdev):
                        total = total + mask[d * tdev + t] * seen[d][t, r * TAIL : (r + 1) * TAIL, :].astype(F32)
                outs[k][s, r * TAIL : (r + 1) * TAIL, :] = total.astype(BF16)


def half_kernel(nsrc, *refs):
    sinks = refs[:nsrc]
    per_ref, out_ref, lhs = refs[nsrc:]
    rows, width = sinks[0].shape[1:]
    nev = width // 2
    for k in range(nsrc):
        lhs[k * rows : (k + 1) * rows, :] = sinks[k][0]
    p = per_ref[0, 0, 0].astype(F32)
    q = -turned(p, nev)
    both = jnp.concatenate([p, q], axis=0).astype(BF16)
    h = jnp.dot(lhs[...], both, preferred_element_type=F32).astype(BF16)
    for k in range(nsrc):
        out_ref[k, 0, 0] = h[k * rows : (k + 1) * rows, :]


def block_kernel(nsrc, index_ref, half_ref, *refs):
    del index_ref
    mine = refs[:nsrc]
    other = refs[nsrc : 2 * nsrc]
    out_ref, rhs = refs[2 * nsrc :]
    rows, width = mine[0].shape[1:]
    nev = width // 2
    slab = lax.axis_index("slab")
    k = pl.program_id(0)
    for j in range(nsrc):

        @pl.when(k == j)
        def _():
            rhs[pl.ds(pl.multiple_of(slab * rows, rows), rows), :] = mine[j][0]
            rhs[pl.ds(pl.multiple_of((1 - slab) * rows, rows), rows), :] = other[j][0]

    rhs[nev:, :] = (-turned(rhs[:nev, :].astype(F32), nev)).astype(BF16)
    shape = half_ref.shape
    lhs = half_ref[0, 0].reshape(shape[2] * rows, width)
    out = lax.dot_general(lhs, rhs[...], (((1,), (1,)), ((), ())), preferred_element_type=F32)
    out_ref[...] = out.reshape(out_ref.shape)


def fast(eigvecs, perambulator, momenta, source_times):
    nsrc, nsnk, slabs = (lax.axis_size(a) for a in ("src", "snk", "slab"))
    tdev, count, width = eigvecs.shape
    sdev = source_times.shape[0]
    nq = perambulator.shape[2]
    nev = width // 2
    rows = nev // slabs
    lz = count // (LX * LY) * nsrc * slabs
    src = lax.axis_index("src")

    def swap(x):
        return lax.ppermute(x, "slab", [(0, 1), (1, 0)])

    def cross(x, k):
        return lax.ppermute(x, "src", [(i, i ^ k) for i in range(nsrc)])

    def shift(x, d):
        return lax.ppermute(x, "snk", [(i, (i + d) % nsnk) for i in range(nsnk)])

    scratch = [
        pltpu.VMEM((4, nsrc, LX, 128), F32),
        pltpu.VMEM((8, 128), F32),
        pltpu.VMEM((count, nsrc * width), BF16),
        pltpu.VMEM((width, count), BF16),
        pltpu.VMEM((8, 128), F32),
    ]
    gram_cost = pl.CostEstimate(
        flops=2 * tdev * count * 2 * rows * width * nsrc, bytes_accessed=2 * eigvecs.size, transcendentals=0
    )
    theirs = swap(eigvecs)
    acc = pl.pallas_call(
        functools.partial(gram_kernel, nsrc, slabs, lz, False),
        out_shape=jax.ShapeDtypeStruct((nsrc, tdev, rows, width), F32),
        in_specs=[SMEM, VMEM],
        out_specs=VMEM,
        scratch_shapes=scratch,
        cost_estimate=gram_cost,
        name="gram_own",
    )(momenta, eigvecs)
    pieces = pl.pallas_call(
        functools.partial(gram_kernel, nsrc, slabs, lz, True),
        out_shape=[jax.ShapeDtypeStruct((tdev, rows, width), F32)]
        + [jax.ShapeDtypeStruct((tdev, rows + TAIL, width), BF16)] * (nsrc - 1),
        in_specs=[SMEM, VMEM, VMEM, SMEM],
        out_specs=[VMEM] * nsrc,
        scratch_shapes=scratch,
        cost_estimate=gram_cost,
        name="gram_sibling",
    )(momenta, theirs, acc, source_times)
    got = [cross(pieces[k], k) for k in range(1, nsrc)]
    red = pl.pallas_call(
        sum_kernel,
        out_shape=jax.ShapeDtypeStruct((tdev, rows, width), BF16),
        in_specs=[VMEM] * nsrc,
        out_specs=VMEM,
        name="sum",
    )(pieces[0], *got)
    seen = [red] + [shift(red, d) for d in range(1, nsnk)]
    sinks = [red] + [cross(red, k) for k in range(1, nsrc)]
    picked = pl.pallas_call(
        functools.partial(pick_kernel, nsnk, nsrc),
        out_shape=[jax.ShapeDtypeStruct((sdev, rows, width), BF16)] * nsrc,
        in_specs=[SMEM] + [VMEM] * (nsrc - 1 + nsnk),
        out_specs=[VMEM] * nsrc,
        name="pick",
    )(source_times, *got, *seen)
    mine = [picked[0]] + [cross(picked[k], k) for k in range(1, nsrc)]
    other = [swap(x) for x in mine]

    tq = tdev * nq
    whole = pl.BlockSpec((1, rows, width), lambda t, s, q: (t, 0, 0))
    half = pl.pallas_call(
        functools.partial(half_kernel, nsrc),
        out_shape=jax.ShapeDtypeStruct((nsrc, sdev, tq, rows, width), BF16),
        grid=(tdev, sdev, nq),
        in_specs=[whole] * nsrc
        + [pl.BlockSpec((1, 1, 1, nev, width), lambda t, s, q: (t, s, q, 0, 0))],
        out_specs=pl.BlockSpec((nsrc, 1, 1, rows, width), lambda t, s, q: (0, s, t * nq + q, 0, 0)),
        scratch_shapes=[pltpu.VMEM((nsrc * rows, width), BF16)],
        cost_estimate=pl.CostEstimate(
            flops=4 * tq * sdev * nsrc * rows * width * width // 2,
            bytes_accessed=2 * perambulator.size,
            transcendentals=0,
        ),
        name="half",
    )(*sinks, perambulator)
    spec = pl.BlockSpec((1, rows, width), lambda k, s, i: (s, 0, 0))
    blocks = pl.pallas_call(
        functools.partial(block_kernel, nsrc),
        out_shape=jax.ShapeDtypeStruct((nsrc, tdev, sdev, nq, rows, width), F32),
        grid_spec=pltpu.PrefetchScalarGridSpec(
            num_scalar_prefetch=1,
            grid=(nsrc, sdev),
            in_specs=[pl.BlockSpec((1, 1, tq, rows, width), lambda k, s, i: (k, s, 0, 0, 0))]
            + [spec] * (2 * nsrc),
            out_specs=pl.BlockSpec(
                (1, tdev, 1, nq, rows, width), lambda k, s, i: (i[0] ^ k, 0, s, 0, 0, 0)
            ),
            scratch_shapes=[pltpu.VMEM((width, width), BF16)],
        ),
        name="blocks",
    )(src.astype(jnp.int32).reshape(1), half, *mine, *other)
    return blocks


def local(eigvecs, perambulator, momenta, source_times):
    nsrc = lax.axis_size("src")
    fits = (
        lax.axis_size("slab") == 2
        and momenta.shape[0] == nsrc
        and nsrc & (nsrc - 1) == 0
        and eigvecs.shape[1] == LX * LY
        and source_times.shape[0] == eigvecs.shape[0]
    )
    return (fast if fits else general)(eigvecs, perambulator, momenta, source_times)


def solution(mesh):
    placed = (P("snk", ("src", "slab"), None), P("snk", "src", None, None, None), P(), P("src"))
    return jax.shard_map(
        local,
        mesh=mesh,
        in_specs=placed,
        out_specs=P(None, "snk", "src", None, "slab", None),
        check_vma=False,
    )
```

time: 186 us -> 100 us (0.54)
  waiting for transfers between devices: 85.3 us -> 24.3 us
  Pallas kernels: 0 us -> 53.7 us
  other arithmetic: 41.1 us -> 0 us
  matrix products: 19.4 us -> 0 us
  starting transfers between devices: 0.3 us -> 16.7 us
  between operations: 13.3 us -> 0.12 us
  local copies, waits for them, and re-layouts: 16.3 us -> 4.61 us
  blocking collectives: 10.6 us -> 0 us
    pallas_call x0 -> x6, Pallas kernels: none -> 53.7 us  [the longest x1 13.3 us: fast(): pl.pallas_call(functools.partial(half_kernel, nsrc), out_shape=jax.ShapeD...]
    reduce_scatter x2 -> x0, waiting for transfers between devices: 45.8 us -> none  [the longest x1 32.9 us: local(): lax.psum_scatter(slab_part, 'src', scatter_dimension=2, tiled=True)]
    psum x1 -> x0, waiting for transfers between devices: 38.6 us -> none  [local(): picked = lax.psum(term.astype(jnp.bfloat16), 'snk')]
    ppermute x0 -> x17, waiting for transfers between devices: none -> 24.3 us  [the longest x9 15.7 us: cross(): return lax.ppermute(x, 'src', [(i, i ^ k) for i in range(nsrc)])]
    dot_general x7 -> x0, matrix products: 19.4 us -> none  [the longest x1 10.2 us: local(): jnp.einsum('mtsqrb,smcb->mtsqrc', half, both, preferred_element_type=jnp....]
    ppermute x0 -> x17, starting transfers between devices: none -> 16.7 us  [the longest x9 11.6 us: cross(): return lax.ppermute(x, 'src', [(i, i ^ k) for i in range(nsrc)])]
    add x7 -> x0, other arithmetic: 16.2 us -> none  [the longest x1 15.1 us: local(): dreal = quad[..., :rows, :nev] + quad[..., rows:, nev:]]
    another operation x8 -> x0, other arithmetic: 13.5 us -> none
  transfers between devices with their start and end apart: 4 -> 17, of which waited for: 4 -> 8; matrix products, arithmetic and copies ran while one was open for 5% -> 0% of each run, Pallas kernels for 0% -> 28%
where the time goes in v1:
time: 100 us; the launch traced here: 99.4 us
  Pallas kernels  53.7 us (54%)
  waiting for transfers between devices  24.3 us (24%)
  starting transfers between devices  16.7 us (17%)
  local copies, waits for them, and re-layouts  4.61 us (5%)
    ppermute x9, waiting for transfers between devices, cross(): return lax.ppermute(x, 'src', [(i, i ^ k) for i in range(nsrc)])  15.7 us
    pallas_call x1, Pallas kernels, fast(): pl.pallas_call(functools.partial(half_kernel, nsrc), out_shape=jax.ShapeD...  13.3 us
    pallas_call x1, Pallas kernels, fast(): pl.pallas_call(functools.partial(gram_kernel, nsrc, slabs, lz, True), out...  11.9 us
    pallas_call x1, Pallas kernels, fast(): pl.pallas_call(functools.partial(gram_kernel, nsrc, slabs, lz, False), ou...  11.9 us
    pallas_call x1, Pallas kernels, fast(): pl.pallas_call(functools.partial(block_kernel, nsrc), out_shape=jax.Shape...  11.7 us
    ppermute x9, starting transfers between devices, cross(): return lax.ppermute(x, 'src', [(i, i ^ k) for i in range(nsrc)])  11.6 us
    ppermute x3, waiting for transfers between devices, shift(): return lax.ppermute(x, 'snk', [(i, (i + d) % nsnk) for i in range(nsnk)])  8.59 us
    unnamed x34, local copies, waits for them, and re-layouts  4.61 us
  transfers between devices with their start and end apart: 17, of which 8 were waited for; matrix products, arithmetic and copies ran while one was open for 0% of the time, Pallas kernels for 28%

profile of v1, /device:TPU:0, one launch (start us, length us, event | category | flops | bytes accessed | tf_op | source)
XLA Modules:
  0.0 99.4 jit_solution(11844447547658199603)
XLA Ops:
  0.5 11.9 %gram_own.1.refs_0_ = f32[4,2,96,384]{3,2,1,0:T(8,128)} custom-call(s32[4,3]{1,0:T(4,128)} %mom_ref.3, bf16[2,1024,384]{2,1,0:T(8,128)(2,1)} %eig_ref.1), custom_call_target="tpu_custom_call" | custom-call | flops 1207959552 | bytes 1572864 | tf_op jit(solution)/shard_map/gram_own/pallas_call | solution.py:243
  12.4 1.1 %copy-done.16 = bf16[2,1024,384]{2,1,0:T(8,128)(2,1)} copy-done((bf16[2,1024,384]{2,1,0:T(8,128)(2,1)}, bf16[2,1024,384]{2,1,0:T(8,128)(2,1)S(1)}, u32[]{:S(2)}) %copy-start.16) | copy-done | bytes 1572888
  13.5 11.9 %gram_sibling.1 = (f32[2,96,384]{2,1,0:T(8,128)}, bf16[2,112,384]{2,1,0:T(8,128)(2,1)}, bf16[2,112,384]{2,1,0:T(8,128)(2,1)}, bf16[2,112,384]{2,1,0:T(8,128)(2,1)}) custom-call(s32[4,3]{1,0:T(4,128)} %mom_ref.3, bf16[2,1024,384]{2,1,0:T(8,128)(2,1)} %copy-done.16, f32[4,2,96,384]{3,2,1,0:T(8,128)} %gram_own.1.refs_0_, s32[2]{0:T(128)} %times_ref.1), custom_call_target="tpu_custom_call" | custom-call | flops 1207959552 | bytes 1572864 | tf_op jit(solution)/shard_map/gram_sibling/pallas_call | solution.py:252
  25.5 2.5 %collective-permute-start.1 = (bf16[2,112,384]{2,1,0:T(8,128)(2,1)}, bf16[2,112,384]{2,1,0:T(8,128)(2,1)S(1)}, u32[]{:S(2)}, u32[]{:S(2)}) collective-permute-start(bf16[2,112,384]{2,1,0:T(8,128)(2,1)} %get-tuple-element.14), channel_id=1, source_target_pairs={{0,8},{8,0},{16,24},{24,16},{1,9},{9,1},{17,25},{25,17},{2,10},{10... | collective-permute-start | bytes 516104 | tf_op jit(solution)/shard_map/ppermute | solution.py:227
  27.9 1.5 %collective-permute-start.2 = (bf16[2,112,384]{2,1,0:T(8,128)(2,1)}, bf16[2,112,384]{2,1,0:T(8,128)(2,1)S(1)}, u32[]{:S(2)}, u32[]{:S(2)}) collective-permute-start(bf16[2,112,384]{2,1,0:T(8,128)(2,1)} %get-tuple-element.15), channel_id=1, source_target_pairs={{0,16},{8,24},{16,0},{24,8},{1,17},{9,25},{17,1},{25,9},{2,18},{10... | collective-permute-start | bytes 516104 | tf_op jit(solution)/shard_map/ppermute | solution.py:227
  29.4 3.9 %collective-permute-done.1.refs_0_ = bf16[2,112,384]{2,1,0:T(8,128)(2,1)S(1)} collective-permute-done((bf16[2,112,384]{2,1,0:T(8,128)(2,1)}, bf16[2,112,384]{2,1,0:T(8,128)(2,1)S(1)}, u32[]{:S(2)}, u32[]{:S(2)}) %collective-permute-start.1) | collective-permute-done | bytes 172064 | tf_op jit(solution)/shard_map/ppermute | solution.py:227
  33.4 5.0 %collective-permute-done.2.refs_1_ = bf16[2,112,384]{2,1,0:T(8,128)(2,1)S(1)} collective-permute-done((bf16[2,112,384]{2,1,0:T(8,128)(2,1)}, bf16[2,112,384]{2,1,0:T(8,128)(2,1)S(1)}, u32[]{:S(2)}, u32[]{:S(2)}) %collective-permute-start.2) | collective-permute-done | bytes 172064 | tf_op jit(solution)/shard_map/ppermute | solution.py:227
  39.1 1.9 %sum.1.refs_0_.refs_3_ = bf16[2,96,384]{2,1,0:T(8,128)(2,1)} custom-call(f32[2,96,384]{2,1,0:T(8,128)} %get-tuple-element.13.own, bf16[2,112,384]{2,1,0:T(8,128)(2,1)} %copy-done, bf16[2,112,384]{2,1,0:T(8,128)(2,1)} %copy-done.1, bf16[2,112,384]{2,1,0:T(8,128)(2,1)} %copy-done.2), custom_call_target="tpu_custom_call" | custom-call | tf_op jit(solution)/shard_map/sum/pallas_call | solution.py:263
  41.0 3.6 %collective-permute-start.9 = (bf16[2,96,384]{2,1,0:T(8,128)(2,1)}, bf16[2,96,384]{2,1,0:T(8,128)(2,1)S(1)}, u32[]{:S(2)}, u32[]{:S(2)}) collective-permute-start(bf16[2,96,384]{2,1,0:T(8,128)(2,1)} %sum.1.refs_0_.refs_3_), channel_id=1, source_target_pairs={{0,6},{2,0},{4,2},{6,4},{1,7},{3,1},{5,3},{7,5},{8,14},{10,8},{12,... | collective-permute-start | bytes 442376 | tf_op jit(solution)/shard_map/ppermute | solution.py:230
  44.6 1.0 %collective-permute-start.7 = (bf16[2,96,384]{2,1,0:T(8,128)(2,1)}, bf16[2,96,384]{2,1,0:T(8,128)(2,1)S(1)}, u32[]{:S(2)}, u32[]{:S(2)}) collective-permute-start(bf16[2,96,384]{2,1,0:T(8,128)(2,1)} %sum.1.refs_0_.refs_3_), channel_id=1, source_target_pairs={{0,2},{2,4},{4,6},{6,0},{1,3},{3,5},{5,7},{7,1},{8,10},{10,12},{12... | collective-permute-start | bytes 442376 | tf_op jit(solution)/shard_map/ppermute | solution.py:230
  45.6 1.5 %collective-permute-start.6 = (bf16[2,96,384]{2,1,0:T(8,128)(2,1)}, bf16[2,96,384]{2,1,0:T(8,128)(2,1)S(1)}, u32[]{:S(2)}, u32[]{:S(2)}) collective-permute-start(bf16[2,96,384]{2,1,0:T(8,128)(2,1)} %sum.1.refs_0_.refs_3_), channel_id=1, source_target_pairs={{0,24},{8,16},{16,8},{24,0},{1,25},{9,17},{17,9},{25,1},{2,26},{10... | collective-permute-start | bytes 442376 | tf_op jit(solution)/shard_map/ppermute | solution.py:227
  47.1 1.2 %collective-permute-start.5 = (bf16[2,96,384]{2,1,0:T(8,128)(2,1)}, bf16[2,96,384]{2,1,0:T(8,128)(2,1)S(1)}, u32[]{:S(2)}, u32[]{:S(2)}) collective-permute-start(bf16[2,96,384]{2,1,0:T(8,128)(2,1)} %sum.1.refs_0_.refs_3_), channel_id=1, source_target_pairs={{0,16},{8,24},{16,0},{24,8},{1,17},{9,25},{17,1},{25,9},{2,18},{10... | collective-permute-start | bytes 442376 | tf_op jit(solution)/shard_map/ppermute | solution.py:227
  48.2 0.9 collective-permute-done.9.refs_6_
  49.1 7.7 %collective-permute-done.8.refs_5_ = bf16[2,96,384]{2,1,0:T(8,128)(2,1)S(1)} collective-permute-done((bf16[2,96,384]{2,1,0:T(8,128)(2,1)}, bf16[2,96,384]{2,1,0:T(8,128)(2,1)S(1)}, u32[]{:S(2)}, u32[]{:S(2)}) %collective-permute-start.8) | collective-permute-done | bytes 147488 | tf_op jit(solution)/shard_map/ppermute | solution.py:230
  58.1 3.0 %pick.1 = (bf16[2,96,384]{2,1,0:T(8,128)(2,1)}, bf16[2,96,384]{2,1,0:T(8,128)(2,1)}, bf16[2,96,384]{2,1,0:T(8,128)(2,1)}, bf16[2,96,384]{2,1,0:T(8,128)(2,1)}) custom-call(s32[2]{0:T(128)} %times_ref.1, bf16[2,112,384]{2,1,0:T(8,128)(2,1)} %copy-done, bf16[2,112,384]{2,1,0:T(8,128)(2,1)} %copy-done.1, bf16[2,112,384]{2,1,0:T(8,128)(2,1)} %copy-done.2, ...), custom_call_target="tpu_custom_call" | custom-call | tf_op jit(solution)/shard_map/pick/pallas_call | solution.py:272
  61.1 1.5 %collective-permute-start.10 = (bf16[2,96,384]{2,1,0:T(8,128)(2,1)}, bf16[2,96,384]{2,1,0:T(8,128)(2,1)S(1)}, u32[]{:S(2)}, u32[]{:S(2)}) collective-permute-start(bf16[2,96,384]{2,1,0:T(8,128)(2,1)} %get-tuple-element.18), channel_id=1, source_target_pairs={{0,8},{8,0},{16,24},{24,16},{1,9},{9,1},{17,25},{25,17},{2,10},{10... | collective-permute-start | bytes 442376 | tf_op jit(solution)/shard_map/ppermute | solution.py:227
  63.2 1.4 %collective-permute-start.12 = (bf16[2,96,384]{2,1,0:T(8,128)(2,1)}, bf16[2,96,384]{2,1,0:T(8,128)(2,1)S(1)}, u32[]{:S(2)}, u32[]{:S(2)}) collective-permute-start(bf16[2,96,384]{2,1,0:T(8,128)(2,1)} %get-tuple-element.20), channel_id=1, source_target_pairs={{0,24},{8,16},{16,8},{24,0},{1,25},{9,17},{17,9},{25,1},{2,26},{10... | collective-permute-start | bytes 442376 | tf_op jit(solution)/shard_map/ppermute | solution.py:227
  64.6 1.5 %collective-permute-start.4 = (bf16[2,96,384]{2,1,0:T(8,128)(2,1)}, bf16[2,96,384]{2,1,0:T(8,128)(2,1)S(1)}, u32[]{:S(2)}, u32[]{:S(2)}) collective-permute-start(bf16[2,96,384]{2,1,0:T(8,128)(2,1)} %sum.1.refs_0_.refs_3_), channel_id=1, source_target_pairs={{0,8},{8,0},{16,24},{24,16},{1,9},{9,1},{17,25},{25,17},{2,10},{10... | collective-permute-start | bytes 442376 | tf_op jit(solution)/shard_map/ppermute | solution.py:227
  66.1 1.2 %collective-permute-done.10.refs_1_ = bf16[2,96,384]{2,1,0:T(8,128)(2,1)S(1)} collective-permute-done((bf16[2,96,384]{2,1,0:T(8,128)(2,1)}, bf16[2,96,384]{2,1,0:T(8,128)(2,1)S(1)}, u32[]{:S(2)}, u32[]{:S(2)}) %collective-permute-start.10) | collective-permute-done | bytes 147488 | tf_op jit(solution)/shard_map/ppermute | solution.py:227
  67.4 2.3 %collective-permute-done.11.refs_2_ = bf16[2,96,384]{2,1,0:T(8,128)(2,1)S(1)} collective-permute-done((bf16[2,96,384]{2,1,0:T(8,128)(2,1)}, bf16[2,96,384]{2,1,0:T(8,128)(2,1)S(1)}, u32[]{:S(2)}, u32[]{:S(2)}) %collective-permute-start.11) | collective-permute-done | bytes 147488 | tf_op jit(solution)/shard_map/ppermute | solution.py:227
  69.7 2.5 %collective-permute-done.12.refs_3_ = bf16[2,96,384]{2,1,0:T(8,128)(2,1)S(1)} collective-permute-done((bf16[2,96,384]{2,1,0:T(8,128)(2,1)}, bf16[2,96,384]{2,1,0:T(8,128)(2,1)S(1)}, u32[]{:S(2)}, u32[]{:S(2)}) %collective-permute-start.12) | collective-permute-done | bytes 147488 | tf_op jit(solution)/shard_map/ppermute | solution.py:227
  72.2 0.7 collective-permute-done.4.refs_1_
  73.6 13.3 %half.1.half_ref = bf16[4,2,8,96,384]{4,3,2,1,0:T(8,128)(2,1)} custom-call(bf16[2,96,384]{2,1,0:T(8,128)(2,1)} %sum.1.refs_0_.refs_3_, bf16[2,96,384]{2,1,0:T(8,128)(2,1)} %copy-done.15, bf16[2,96,384]{2,1,0:T(8,128)(2,1)} %copy-done.14, bf16[2,96,384]{2,1,0:T(8,128)(2,1)} %copy-done.13, bf16[2,2,4,192,384]{4,3,2,1,0:T(8,128)(2,1)} %refs_4_.1), custom_call_target="tpu_custom_call" | custom-call | flops 1811939328 | bytes 2359296 | tf_op jit(solution)/shard_map/half/pallas_call | solution.py:284
  87.7 11.7 %blocks.1 = f32[4,2,2,4,96,384]{5,4,3,2,1,0:T(8,128)} custom-call(s32[1]{0:T(128)} %bitcast.index_ref, bf16[4,2,8,96,384]{4,3,2,1,0:T(8,128)(2,1)} %half.1.half_ref, bf16[2,96,384]{2,1,0:T(8,128)(2,1)} %get-tuple-element.17.refs_0_, bf16[2,96,384]{2,1,0:T(8,128)(2,1)} %copy-done.3, bf16[2,96,384]{2,1,0:T(8,128)(2,1)} %copy-done.4, ...), custom_call_target="tpu_custom_call" | custom-call | tf_op jit(solution)/shard_map/blocks/pallas_call | solution.py:300
  (50 shorter events, 4.6 us)
Async XLA Ops:
  0.0 12.4 %collective-permute-start = (bf16[2,1024,384]{2,1,0:T(8,128)(2,1)}, bf16[2,1024,384]{2,1,0:T(8,128)(2,1)S(1)}, u32[]{:S(2)}, u32[]{:S(2)}) collective-permute-start(bf16[2,1024,384]{2,1,0:T(8,128)(2,1)} %eig_ref.1), channel_id=1, source_target_pairs={{0,1},{1,0},{2,3},{3,2},{4,5},{5,4},{6,7},{7,6},{8,9},{9,8},{10,11... | collective-permute-start | bytes 4718600 | tf_op jit(solution)/shard_map/ppermute | solution.py:224
  25.5 7.9 %collective-permute-start.1 = (bf16[2,112,384]{2,1,0:T(8,128)(2,1)}, bf16[2,112,384]{2,1,0:T(8,128)(2,1)S(1)}, u32[]{:S(2)}, u32[]{:S(2)}) collective-permute-start(bf16[2,112,384]{2,1,0:T(8,128)(2,1)} %get-tuple-element.14), channel_id=1, source_target_pairs={{0,8},{8,0},{16,24},{24,16},{1,9},{9,1},{17,25},{25,17},{2,10},{10... | collective-permute-start | bytes 516104 | tf_op jit(solution)/shard_map/ppermute | solution.py:227
  27.9 10.4 %collective-permute-start.2 = (bf16[2,112,384]{2,1,0:T(8,128)(2,1)}, bf16[2,112,384]{2,1,0:T(8,128)(2,1)S(1)}, u32[]{:S(2)}, u32[]{:S(2)}) collective-permute-start(bf16[2,112,384]{2,1,0:T(8,128)(2,1)} %get-tuple-element.15), channel_id=1, source_target_pairs={{0,16},{8,24},{16,0},{24,8},{1,17},{9,25},{17,1},{25,9},{2,18},{10... | collective-permute-start | bytes 516104 | tf_op jit(solution)/shard_map/ppermute | solution.py:227
  29.4 8.9 %collective-permute-start.3 = (bf16[2,112,384]{2,1,0:T(8,128)(2,1)}, bf16[2,112,384]{2,1,0:T(8,128)(2,1)S(1)}, u32[]{:S(2)}, u32[]{:S(2)}) collective-permute-start(bf16[2,112,384]{2,1,0:T(8,128)(2,1)} %get-tuple-element.16), channel_id=1, source_target_pairs={{0,24},{8,16},{16,8},{24,0},{1,25},{9,17},{17,9},{25,1},{2,26},{10... | collective-permute-start | bytes 516104 | tf_op jit(solution)/shard_map/ppermute | solution.py:227
  33.4 5.0 %copy-start = (bf16[2,112,384]{2,1,0:T(8,128)(2,1)}, bf16[2,112,384]{2,1,0:T(8,128)(2,1)S(1)}, u32[]{:S(2)}) copy-start(bf16[2,112,384]{2,1,0:T(8,128)(2,1)S(1)} %collective-permute-done.1.refs_0_) | copy-start | bytes 516100
  41.0 8.1 %collective-permute-start.9 = (bf16[2,96,384]{2,1,0:T(8,128)(2,1)}, bf16[2,96,384]{2,1,0:T(8,128)(2,1)S(1)}, u32[]{:S(2)}, u32[]{:S(2)}) collective-permute-start(bf16[2,96,384]{2,1,0:T(8,128)(2,1)} %sum.1.refs_0_.refs_3_), channel_id=1, source_target_pairs={{0,6},{2,0},{4,2},{6,4},{1,7},{3,1},{5,3},{7,5},{8,14},{10,8},{12,... | collective-permute-start | bytes 442376 | tf_op jit(solution)/shard_map/ppermute | solution.py:230
  44.6 12.3 %collective-permute-start.8 = (bf16[2,96,384]{2,1,0:T(8,128)(2,1)}, bf16[2,96,384]{2,1,0:T(8,128)(2,1)S(1)}, u32[]{:S(2)}, u32[]{:S(2)}) collective-permute-start(bf16[2,96,384]{2,1,0:T(8,128)(2,1)} %sum.1.refs_0_.refs_3_), channel_id=1, source_target_pairs={{0,4},{2,6},{4,0},{6,2},{1,5},{3,7},{5,1},{7,3},{8,12},{10,14},{12... | collective-permute-start | bytes 442376 | tf_op jit(solution)/shard_map/ppermute | solution.py:230
  44.6 12.3 %collective-permute-start.7 = (bf16[2,96,384]{2,1,0:T(8,128)(2,1)}, bf16[2,96,384]{2,1,0:T(8,128)(2,1)S(1)}, u32[]{:S(2)}, u32[]{:S(2)}) collective-permute-start(bf16[2,96,384]{2,1,0:T(8,128)(2,1)} %sum.1.refs_0_.refs_3_), channel_id=1, source_target_pairs={{0,2},{2,4},{4,6},{6,0},{1,3},{3,5},{5,7},{7,1},{8,10},{10,12},{12... | collective-permute-start | bytes 442376 | tf_op jit(solution)/shard_map/ppermute | solution.py:230
  45.6 19.1 %collective-permute-start.6 = (bf16[2,96,384]{2,1,0:T(8,128)(2,1)}, bf16[2,96,384]{2,1,0:T(8,128)(2,1)S(1)}, u32[]{:S(2)}, u32[]{:S(2)}) collective-permute-start(bf16[2,96,384]{2,1,0:T(8,128)(2,1)} %sum.1.refs_0_.refs_3_), channel_id=1, source_target_pairs={{0,24},{8,16},{16,8},{24,0},{1,25},{9,17},{17,9},{25,1},{2,26},{10... | collective-permute-start | bytes 442376 | tf_op jit(solution)/shard_map/ppermute | solution.py:227
  47.1 19.0 %collective-permute-start.5 = (bf16[2,96,384]{2,1,0:T(8,128)(2,1)}, bf16[2,96,384]{2,1,0:T(8,128)(2,1)S(1)}, u32[]{:S(2)}, u32[]{:S(2)}) collective-permute-start(bf16[2,96,384]{2,1,0:T(8,128)(2,1)} %sum.1.refs_0_.refs_3_), channel_id=1, source_target_pairs={{0,16},{8,24},{16,0},{24,8},{1,17},{9,25},{17,1},{25,9},{2,18},{10... | collective-permute-start | bytes 442376 | tf_op jit(solution)/shard_map/ppermute | solution.py:227
  49.1 7.7 %copy-start.10 = (bf16[2,96,384]{2,1,0:T(8,128)(2,1)}, bf16[2,96,384]{2,1,0:T(8,128)(2,1)S(1)}, u32[]{:S(2)}) copy-start(bf16[2,96,384]{2,1,0:T(8,128)(2,1)S(1)} %collective-permute-done.9.refs_6_) | copy-start | bytes 442372
  61.1 6.2 %collective-permute-start.10 = (bf16[2,96,384]{2,1,0:T(8,128)(2,1)}, bf16[2,96,384]{2,1,0:T(8,128)(2,1)S(1)}, u32[]{:S(2)}, u32[]{:S(2)}) collective-permute-start(bf16[2,96,384]{2,1,0:T(8,128)(2,1)} %get-tuple-element.18), channel_id=1, source_target_pairs={{0,8},{8,0},{16,24},{24,16},{1,9},{9,1},{17,25},{25,17},{2,10},{10... | collective-permute-start | bytes 442376 | tf_op jit(solution)/shard_map/ppermute | solution.py:227
  62.6 7.1 %collective-permute-start.11 = (bf16[2,96,384]{2,1,0:T(8,128)(2,1)}, bf16[2,96,384]{2,1,0:T(8,128)(2,1)S(1)}, u32[]{:S(2)}, u32[]{:S(2)}) collective-permute-start(bf16[2,96,384]{2,1,0:T(8,128)(2,1)} %get-tuple-element.19), channel_id=1, source_target_pairs={{0,16},{8,24},{16,0},{24,8},{1,17},{9,25},{17,1},{25,9},{2,18},{10... | collective-permute-start | bytes 442376 | tf_op jit(solution)/shard_map/ppermute | solution.py:227
  63.2 9.0 %collective-permute-start.12 = (bf16[2,96,384]{2,1,0:T(8,128)(2,1)}, bf16[2,96,384]{2,1,0:T(8,128)(2,1)S(1)}, u32[]{:S(2)}, u32[]{:S(2)}) collective-permute-start(bf16[2,96,384]{2,1,0:T(8,128)(2,1)} %get-tuple-element.20), channel_id=1, source_target_pairs={{0,24},{8,16},{16,8},{24,0},{1,25},{9,17},{17,9},{25,1},{2,26},{10... | collective-permute-start | bytes 442376 | tf_op jit(solution)/shard_map/ppermute | solution.py:227
  64.6 8.3 %copy-start.13 = (bf16[2,96,384]{2,1,0:T(8,128)(2,1)}, bf16[2,96,384]{2,1,0:T(8,128)(2,1)S(1)}, u32[]{:S(2)}) copy-start(bf16[2,96,384]{2,1,0:T(8,128)(2,1)S(1)} %collective-permute-done.6.refs_3_) | copy-start | bytes 442372
  64.6 8.3 %collective-permute-start.4 = (bf16[2,96,384]{2,1,0:T(8,128)(2,1)}, bf16[2,96,384]{2,1,0:T(8,128)(2,1)S(1)}, u32[]{:S(2)}, u32[]{:S(2)}) collective-permute-start(bf16[2,96,384]{2,1,0:T(8,128)(2,1)} %sum.1.refs_0_.refs_3_), channel_id=1, source_target_pairs={{0,8},{8,0},{16,24},{24,16},{1,9},{9,1},{17,25},{25,17},{2,10},{10... | collective-permute-start | bytes 442376 | tf_op jit(solution)/shard_map/ppermute | solution.py:227
  66.1 6.8 %copy-start.14 = (bf16[2,96,384]{2,1,0:T(8,128)(2,1)}, bf16[2,96,384]{2,1,0:T(8,128)(2,1)S(1)}, u32[]{:S(2)}) copy-start(bf16[2,96,384]{2,1,0:T(8,128)(2,1)S(1)} %collective-permute-done.5.refs_2_) | copy-start | bytes 442372
  66.1 20.8 %collective-permute-start.13 = (bf16[2,96,384]{2,1,0:T(8,128)(2,1)}, bf16[2,96,384]{2,1,0:T(8,128)(2,1)S(1)}, u32[]{:S(2)}, u32[]{:S(2)}) collective-permute-start(bf16[2,96,384]{2,1,0:T(8,128)(2,1)} %get-tuple-element.17.refs_0_), channel_id=1, source_target_pairs={{0,1},{1,0},{2,3},{3,2},{4,5},{5,4},{6,7},{7,6},{8,9},{9,8},{10,11... | collective-permute-start | bytes 442376 | tf_op jit(solution)/shard_map/ppermute | solution.py:224
  67.4 19.5 %copy-start.3 = (bf16[2,96,384]{2,1,0:T(8,128)(2,1)}, bf16[2,96,384]{2,1,0:T(8,128)(2,1)S(1)}, u32[]{:S(2)}) copy-start(bf16[2,96,384]{2,1,0:T(8,128)(2,1)S(1)} %collective-permute-done.10.refs_1_) | copy-start | bytes 442372
  67.4 19.6 %collective-permute-start.14 = (bf16[2,96,384]{2,1,0:T(8,128)(2,1)S(1)}, bf16[2,96,384]{2,1,0:T(8,128)(2,1)S(1)}, u32[]{:S(2)}, u32[]{:S(2)}) collective-permute-start(bf16[2,96,384]{2,1,0:T(8,128)(2,1)S(1)} %collective-permute-done.10.refs_1_), channel_id=1, source_target_pairs={{0,1},{1,0},{2,3},{3,2},{4,5},{5,4},{6,7},{7,6},{8,9},{9,8},{10,11... | collective-permute-start | bytes 442376 | tf_op jit(solution)/shard_map/ppermute | solution.py:224
  69.7 17.2 %copy-start.4 = (bf16[2,96,384]{2,1,0:T(8,128)(2,1)}, bf16[2,96,384]{2,1,0:T(8,128)(2,1)S(1)}, u32[]{:S(2)}) copy-start(bf16[2,96,384]{2,1,0:T(8,128)(2,1)S(1)} %collective-permute-done.11.refs_2_) | copy-start | bytes 442372
  69.7 17.2 %collective-permute-start.15 = (bf16[2,96,384]{2,1,0:T(8,128)(2,1)S(1)}, bf16[2,96,384]{2,1,0:T(8,128)(2,1)S(1)}, u32[]{:S(2)}, u32[]{:S(2)}) collective-permute-start(bf16[2,96,384]{2,1,0:T(8,128)(2,1)S(1)} %collective-permute-done.11.refs_2_), channel_id=1, source_target_pairs={{0,1},{1,0},{2,3},{3,2},{4,5},{5,4},{6,7},{7,6},{8,9},{9,8},{10,11... | collective-permute-start | bytes 442376 | tf_op jit(solution)/shard_map/ppermute | solution.py:224
  72.2 14.7 %copy-start.5 = (bf16[2,96,384]{2,1,0:T(8,128)(2,1)}, bf16[2,96,384]{2,1,0:T(8,128)(2,1)S(1)}, u32[]{:S(2)}) copy-start(bf16[2,96,384]{2,1,0:T(8,128)(2,1)S(1)} %collective-permute-done.12.refs_3_) | copy-start | bytes 442372
  72.2 14.8 %collective-permute-start.16 = (bf16[2,96,384]{2,1,0:T(8,128)(2,1)S(1)}, bf16[2,96,384]{2,1,0:T(8,128)(2,1)S(1)}, u32[]{:S(2)}, u32[]{:S(2)}) collective-permute-start(bf16[2,96,384]{2,1,0:T(8,128)(2,1)S(1)} %collective-permute-done.12.refs_3_), channel_id=1, source_target_pairs={{0,1},{1,0},{2,3},{3,2},{4,5},{5,4},{6,7},{7,6},{8,9},{9,8},{10,11... | collective-permute-start | bytes 442376 | tf_op jit(solution)/shard_map/ppermute | solution.py:224
  (10 other events, 7.3 us)

commit v2 on v0

v2 whole, which is shorter than its diff:
```python
import functools
import math

import jax
import jax.numpy as jnp
from jax import lax
from jax.experimental import pallas as pl
from jax.experimental.pallas import tpu as pltpu
from jax.sharding import PartitionSpec as P


LX = 32
LY = 32
TAIL = 16
F32 = jnp.float32
BF16 = jnp.bfloat16
VMEM = pl.BlockSpec(memory_space=pltpu.VMEM)
SMEM = pl.BlockSpec(memory_space=pltpu.SMEM)


def angles(momenta, xs, ys, zs, lz):
    fx = (momenta[:, 0:1] * xs[None, :] % LX).astype(F32) / LX
    fy = (momenta[:, 1:2] * ys[None, :] % LY).astype(F32) / LY
    fz = (momenta[:, 2:3] * zs[None, :] % lz).astype(F32) / lz
    return 2.0 * math.pi * (fx + fy + fz)


def general(eigvecs, perambulator, momenta, source_times):
    nev = eigvecs.shape[2] // 2
    count = eigvecs.shape[1]
    zpl = count // (LX * LY)
    slabs = lax.axis_size("slab")
    lz = zpl * lax.axis_size("src") * slabs
    sites = jnp.arange(count, dtype=jnp.int32)
    xs = sites % LX
    ys = sites // LX % LY
    zs = sites // (LX * LY) + lax.axis_index(("src", "slab")) * zpl
    angle = angles(momenta, xs, ys, zs, lz)
    vreal = eigvecs[:, :, :nev].astype(F32)
    vimag = eigvecs[:, :, nev:].astype(F32)
    partials = []
    for m in range(angle.shape[0]):
        cosine = jnp.cos(angle[m])[None, :, None]
        sine = jnp.sin(angle[m])[None, :, None]
        phased = jnp.concatenate(
            [cosine * vreal + sine * vimag, cosine * vimag - sine * vreal], axis=2
        ).astype(BF16)
        gram = jnp.einsum("tsa,tsb->tab", eigvecs, phased, preferred_element_type=F32)
        real = gram[:, :nev, :nev] + gram[:, nev:, nev:]
        imag = gram[:, :nev, nev:] - gram[:, nev:, :nev]
        partials.append(jnp.concatenate([real, imag], axis=2))
    partial_value = jnp.stack(partials, axis=1)
    tdev = partial_value.shape[0]
    rows = nev // slabs
    local_times = lax.axis_index("snk") * tdev + jnp.arange(tdev, dtype=jnp.int32)
    slab_part = lax.psum_scatter(partial_value, "slab", scatter_dimension=2, tiled=True)
    share = lax.psum_scatter(slab_part, "src", scatter_dimension=2, tiled=True).astype(BF16)
    sink = lax.all_gather(share, "src", axis=2, tiled=True)
    selector = (source_times[:, None] == local_times[None, :]).astype(BF16)
    term = jnp.dot(selector, sink.reshape(tdev, -1), preferred_element_type=F32)
    picked = lax.psum(term.astype(BF16), "snk")
    picked = picked.reshape((source_times.shape[0],) + sink.shape[1:])
    source = lax.all_gather(picked, "slab", axis=2, tiled=True)
    stacked = jnp.concatenate([sink[..., :nev], sink[..., nev:]], axis=2)
    prod = jnp.einsum("tmra,tsqab->mtsqrb", stacked, perambulator, preferred_element_type=F32)
    creal = prod[..., :rows, :nev] - prod[..., rows:, nev:]
    cimag = prod[..., :rows, nev:] + prod[..., rows:, :nev]
    half = jnp.concatenate([creal, cimag], axis=4).astype(BF16)
    both = jnp.concatenate([source[..., :nev], source[..., nev:]], axis=2)
    quad = jnp.einsum("mtsqrb,smcb->mtsqrc", half, both, preferred_element_type=F32)
    dreal = quad[..., :rows, :nev] + quad[..., rows:, nev:]
    dimag = quad[..., rows:, :nev] - quad[..., :rows, nev:]
    return jnp.concatenate([dreal, dimag], axis=-1)


def turned(x, nev):
    return jnp.concatenate([x[:, nev:], -x[:, :nev]], axis=1)


def circle(f):
    turns = jnp.floor(4.0 * f + 0.5)
    r = (f - 0.25 * turns) * (2.0 * math.pi)
    n = turns.astype(jnp.int32) & 3
    x = r * r
    c = 1.0 + x * (-1 / 2 + x * (1 / 24 + x * (-1 / 720 + x * (1 / 40320))))
    s = r * (1.0 + x * (-1 / 6 + x * (1 / 120 + x * (-1 / 5040 + x * (1 / 362880)))))
    odd = (n & 1) == 1
    cosine = jnp.where(odd, s, c)
    sine = jnp.where(odd, c, s)
    return (
        jnp.where((n == 1) | (n == 2), -cosine, cosine),
        jnp.where(n >= 2, -sine, sine),
    )


def phases(pieces, z, lz, mom_ref, tab):
    src = lax.axis_index("src")
    index = lax.broadcasted_iota(jnp.int32, (LX, 128), 0)
    for i, k in enumerate(pieces):
        m = src ^ k
        tab[0, i], tab[1, i] = circle((mom_ref[m, 0] * index % LX).astype(F32) / LX)
        fz = (mom_ref[m, 2] * z % lz).astype(F32) / lz
        tab[2, i], tab[3, i] = circle((mom_ref[m, 1] * index % LY).astype(F32) / LY + fz)


def spread(pieces, vec, tab, wide):
    count, width = vec.shape
    nev = width // 2

    def step(y, _):
        at = pl.multiple_of(y * LX, LX)
        v = vec[pl.ds(at, LX), :].astype(F32)
        u = turned(v, nev)
        for i in range(len(pieces)):
            cy = jnp.broadcast_to(tab[2, i, pl.ds(y, 1), :], (LX, 128))
            sy = jnp.broadcast_to(tab[3, i, pl.ds(y, 1), :], (LX, 128))
            cx, sx = tab[0, i], tab[1, i]
            c = jnp.concatenate([cx * cy - sx * sy] * (width // 128), axis=1)
            s = jnp.concatenate([sx * cy + cx * sy] * (width // 128), axis=1)
            wide[pl.ds(at, LX), i * width : (i + 1) * width] = (c * v + s * u).astype(BF16)
        return 0

    lax.fori_loop(0, count // LX, step, 0, unroll=2)


def gather_rows(pieces, vec, tab, wide, tran, add):
    width = vec.shape[1]
    nev = width // 2
    spread(pieces, vec, tab, wide)
    tran[...] = vec[...].T
    for i, k in enumerate(pieces):
        g = jnp.dot(tran[...], wide[:, i * width : (i + 1) * width], preferred_element_type=F32)
        add(i, k, g[:nev] + turned(g[nev:], nev))


def own_kernel(slabs, lz, pieces, mom_hbm, eig_hbm, acc_ref, vec, tab, wide, tran, mom_ref, sem):
    slab = lax.axis_index("slab")
    small = pltpu.make_async_copy(mom_hbm, mom_ref, sem.at[0])
    large = pltpu.make_async_copy(eig_hbm.at[slab], vec, sem.at[1])
    small.start()
    large.start()
    small.wait()
    phases(pieces, lax.axis_index("src") * slabs + slab, lz, mom_ref, tab)
    large.wait()

    def add(i, k, sums):
        acc_ref[i] = sums

    gather_rows(pieces, vec, tab, wide, tran, add)


def sibling_kernel(slabs, lz, pieces, mom_hbm, times_hbm, eig_ref, acc_ref, *refs):
    outs = refs[: len(pieces)]
    tab, wide, tran, mom_ref, times_ref, sem = refs[len(pieces) :]
    width = eig_ref.shape[2]
    nev = width // 2
    slab = lax.axis_index("slab")
    small = pltpu.make_async_copy(mom_hbm, mom_ref, sem.at[0])
    times = pltpu.make_async_copy(times_hbm, times_ref, sem.at[1])
    small.start()
    times.start()
    small.wait()
    phases(pieces, lax.axis_index("src") * slabs + 1 - slab, lz, mom_ref, tab)

    def add(i, k, sums):
        outs[i][:nev, :] = (sums + acc_ref[i]).astype(BF16)

    gather_rows(pieces, eig_ref.at[slab], tab, wide, tran, add)
    times.wait()
    for i in range(len(pieces)):
        for s in range(times_ref.shape[0]):
            time = jnp.full((TAIL, width), times_ref[s].astype(F32), F32)
            outs[i][nev + s * TAIL : nev + (s + 1) * TAIL, :] = time.astype(BF16)


def last_kernel(slabs, lz, mom_hbm, eig_hbm, eig_ref, out, vec, tab, wide, tran, mom_ref, sem):
    slab = lax.axis_index("slab")
    src = lax.axis_index("src")
    small = pltpu.make_async_copy(mom_hbm, mom_ref, sem.at[0])
    large = pltpu.make_async_copy(eig_hbm.at[slab], vec, sem.at[1])
    small.start()
    large.start()
    small.wait()
    phases([0], src * slabs + 1 - slab, lz, mom_ref, tab)

    def put(i, k, sums):
        out[...] = sums

    gather_rows([0], eig_ref.at[slab], tab, wide, tran, put)
    phases([0], src * slabs + slab, lz, mom_ref, tab)
    large.wait()

    def add(i, k, sums):
        out[...] = out[...] + sums

    gather_rows([0], vec, tab, wide, tran, add)


def sum_kernel(own, *refs):
    keep, send = refs[-2:]
    rows = keep.shape[0]
    slab = lax.axis_index("slab")
    for out, part in ((keep, slab), (send, 1 - slab)):
        at = pl.multiple_of(part * rows, rows)
        total = own[pl.ds(at, rows), :]
        for r in refs[:-2]:
            total = total + r[pl.ds(at, rows), :].astype(F32)
        out[...] = total.astype(BF16)


def join_kernel(keep, came, out):
    slab = lax.axis_index("slab")
    out[slab] = keep[...]
    out[1 - slab] = came[...]


def pick_kernel(nsnk, nsrc, times_ref, *refs):
    sent = refs[: nsrc - 1]
    seen = refs[nsrc - 1 : nsrc - 1 + nsnk]
    outs = refs[nsrc - 1 + nsnk :]
    tdev, rows, width = seen[0].shape
    nev = width // 2
    snk = lax.axis_index("snk")
    for k in range(nsrc):
        for s in range(outs[k].shape[0]):
            if k == 0:
                want = jnp.full((TAIL, 128), times_ref[s].astype(F32), F32)
            else:
                want = sent[k - 1][nev + s * TAIL : nev + (s + 1) * TAIL, :128].astype(F32)
            mask = []
            for d in range(nsnk):
                for t in range(tdev):
                    time = ((snk ^ d) * tdev + t).astype(F32)
                    one = (want == time).astype(F32).astype(BF16)
                    mask.append(jnp.concatenate([one] * (width // 128), axis=1))
            for r in range(rows // TAIL):
                total = None
                for d in range(nsnk):
                    for t in range(tdev):
                        term = mask[d * tdev + t] * seen[d][t, r * TAIL : (r + 1) * TAIL, :]
                        total = term if total is None else total + term
                outs[k][s, r * TAIL : (r + 1) * TAIL, :] = total


def half_kernel(nsrc, *refs):
    sinks = refs[:nsrc]
    per_ref, out_ref, lhs, rhs = refs[nsrc:]
    rows, width = sinks[0].shape[1:]
    nev = width // 2
    nq = per_ref.shape[2]
    for k in range(nsrc):
        lhs[k * rows : (k + 1) * rows, :] = sinks[k][0]
    for q in range(nq):
        p = per_ref[0, 0, q]
        rhs[:nev, q * width : (q + 1) * width] = p
        rhs[nev:, q * width : (q + 1) * width] = (-turned(p.astype(F32), nev)).astype(BF16)
    h = jnp.dot(lhs[...], rhs[...], preferred_element_type=F32).astype(BF16)
    for q in range(nq):
        for k in range(nsrc):
            out_ref[k, 0, q] = h[k * rows : (k + 1) * rows, q * width : (q + 1) * width]


def block_kernel(pieces, index_ref, half_ref, *refs):
    del index_ref
    mine = refs[:pieces]
    other = refs[pieces : 2 * pieces]
    out_ref, rhs = refs[-2:]
    rows, width = mine[0].shape[1:]
    nev = width // 2
    slab = lax.axis_index("slab")
    for j in range(pieces):

        @pl.when((pl.program_id(0) == j) & (pl.program_id(2) == 0))
        def _():
            rhs[pl.ds(pl.multiple_of(slab * rows, rows), rows), :] = mine[j][0]
            rhs[pl.ds(pl.multiple_of((1 - slab) * rows, rows), rows), :] = other[j][0]
            rhs[nev:, :] = (-turned(rhs[:nev, :].astype(F32), nev)).astype(BF16)

    nq = half_ref.shape[2]
    lhs = half_ref[0, 0].reshape(nq * rows, width)
    out = lax.dot_general(lhs, rhs[...], (((1,), (1,)), ((), ())), preferred_element_type=F32)
    out_ref[...] = out.reshape(out_ref.shape)


def fast(eigvecs, perambulator, momenta, source_times):
    nsrc, nsnk, slabs = (lax.axis_size(a) for a in ("src", "snk", "slab"))
    tdev, count, width = eigvecs.shape
    sdev = source_times.shape[0]
    nq = perambulator.shape[2]
    nev = width // 2
    rows = nev // slabs
    lz = count // (LX * LY) * nsrc * slabs
    index = lax.axis_index("src").astype(jnp.int32).reshape(1)

    def shape(dims, dtype=BF16):
        return jax.ShapeDtypeStruct(dims, dtype)

    def params(mib):
        return pltpu.CompilerParams(vmem_limit_bytes=mib * 2**20)

    def cost(flops, moved):
        return pl.CostEstimate(flops=flops, bytes_accessed=moved, transcendentals=0)

    def swap(x):
        return lax.ppermute(x, "slab", [(0, 1), (1, 0)])

    def cross(x, k):
        return lax.ppermute(x, "src", [(i, i ^ k) for i in range(nsrc)])

    def along(x, d):
        return lax.ppermute(x, "snk", [(i, i ^ d) for i in range(nsnk)])

    theirs = swap(eigvecs)
    work = 2 * width * count * width
    hbm = pl.BlockSpec(memory_space=pltpu.HBM)
    sent = list(range(nsrc - 1, 0, -1))

    def grams(n, *more):
        return [
            pltpu.VMEM((4, n, LX, 128), F32),
            pltpu.VMEM((count, n * width), BF16),
            pltpu.VMEM((width, count), BF16),
            pltpu.SMEM(momenta.shape, jnp.int32),
            *more,
            pltpu.SemaphoreType.DMA((2,)),
        ]

    vec = pltpu.VMEM((count, width), BF16)
    acc = pl.pallas_call(
        functools.partial(own_kernel, slabs, lz, sent),
        out_shape=shape((len(sent), nev, width), F32),
        in_specs=[hbm, hbm],
        out_specs=VMEM,
        scratch_shapes=[vec] + grams(len(sent)),
        cost_estimate=cost(len(sent) * work, 2 * count * width),
        compiler_params=params(12),
        name="gram_own",
    )(momenta, eigvecs)
    parts = pl.pallas_call(
        functools.partial(sibling_kernel, slabs, lz, sent),
        out_shape=[shape((nev + sdev * TAIL, width))] * len(sent),
        in_specs=[hbm, hbm, VMEM, VMEM],
        out_specs=[VMEM] * len(sent),
        scratch_shapes=grams(len(sent), pltpu.SMEM(source_times.shape, jnp.int32)),
        cost_estimate=cost(len(sent) * work, 2 * count * width),
        compiler_params=params(12),
        name="gram_sibling",
    )(momenta, source_times, theirs, acc)
    got = [cross(part, k) for k, part in zip(sent, parts)][::-1]
    own = pl.pallas_call(
        functools.partial(last_kernel, slabs, lz),
        out_shape=shape((nev, width), F32),
        in_specs=[hbm, hbm, VMEM],
        out_specs=VMEM,
        scratch_shapes=[vec] + grams(1),
        cost_estimate=cost(2 * work, 2 * count * width),
        compiler_params=params(12),
        name="gram_last",
    )(momenta, eigvecs, theirs)
    keep, send = pl.pallas_call(
        sum_kernel,
        out_shape=[shape((rows, width))] * 2,
        in_specs=[VMEM] * nsrc,
        out_specs=[VMEM] * 2,
        compiler_params=params(4),
        name="sum",
    )(own, *got)
    red = pl.pallas_call(
        join_kernel,
        out_shape=shape((tdev, rows, width)),
        in_specs=[VMEM] * 2,
        out_specs=VMEM,
        compiler_params=params(4),
        name="join",
    )(keep, swap(send))
    seen = [red] + [along(red, d) for d in range(1, nsnk)]
    sinks = [red] + [cross(red, k) for k in range(1, nsrc)]
    picked = pl.pallas_call(
        functools.partial(pick_kernel, nsnk, nsrc),
        out_shape=[shape((sdev, rows, width))] * nsrc,
        in_specs=[SMEM] + [VMEM] * (nsrc - 1 + nsnk),
        out_specs=[VMEM] * nsrc,
        compiler_params=params(8),
        name="pick",
    )(source_times, *got, *seen)

    tq = tdev * nq
    per_t = pl.BlockSpec((1, rows, width), lambda t, s: (t, 0, 0))
    half = pl.pallas_call(
        functools.partial(half_kernel, nsrc),
        out_shape=shape((nsrc, sdev, tq, rows, width)),
        grid=(tdev, sdev),
        in_specs=[per_t] * nsrc
        + [pl.BlockSpec((1, 1, nq, nev, width), lambda t, s: (t, s, 0, 0, 0))],
        out_specs=pl.BlockSpec((nsrc, 1, nq, rows, width), lambda t, s: (0, s, t, 0, 0)),
        scratch_shapes=[
            pltpu.VMEM((nsrc * rows, width), BF16),
            pltpu.VMEM((width, nq * width), BF16),
        ],
        cost_estimate=cost(2 * tq * sdev * nsrc * rows * width * width, 2 * perambulator.size),
        compiler_params=params(16),
        name="half",
    )(*sinks, perambulator)

    mine = [picked[0]] + [cross(picked[k], k) for k in range(1, nsrc)]
    other = [swap(x) for x in mine]

    def finish(first, count, before):
        n = count
        chained = before is not None
        return pl.pallas_call(
            functools.partial(block_kernel, n),
            out_shape=shape((nsrc, tdev, sdev, nq, rows, width), F32),
            grid_spec=pltpu.PrefetchScalarGridSpec(
                num_scalar_prefetch=1,
                grid=(n, sdev, tdev),
                in_specs=[
                    pl.BlockSpec(
                        (1, 1, nq, rows, width), lambda k, s, t, i: (first + k, s, t, 0, 0)
                    )
                ]
                + [pl.BlockSpec((1, rows, width), lambda k, s, t, i: (s, 0, 0))] * (2 * n)
                + [pl.BlockSpec(memory_space=pl.ANY)] * chained,
                out_specs=pl.BlockSpec(
                    (1, 1, 1, nq, rows, width),
                    lambda k, s, t, i: (i[0] ^ (first + k), t, s, 0, 0, 0),
                ),
                scratch_shapes=[pltpu.VMEM((width, width), BF16)],
            ),
            input_output_aliases={2 + 2 * n: 0} if chained else {},
            cost_estimate=cost(
                2 * n * tq * sdev * rows * width * width, 4 * n * tq * sdev * rows * width
            ),
            compiler_params=params(12),
        )(
            index,
            half,
            *mine[first : first + n],
            *other[first : first + n],
            *([before] if chained else []),
        )

    blocks = finish(0, 1, None)
    return finish(1, nsrc - 1, blocks)


def local(eigvecs, perambulator, momenta, source_times):
    nsrc = lax.axis_size("src")
    fits = (
        lax.axis_size("slab") == 2
        and momenta.shape[0] == nsrc
        and nsrc & (nsrc - 1) == 0
        and eigvecs.shape[1] == LX * LY
        and source_times.shape[0] == eigvecs.shape[0]
    )
    return (fast if fits else general)(eigvecs, perambulator, momenta, source_times)


def solution(mesh):
    placed = (P("snk", ("src", "slab"), None), P("snk", "src", None, None, None), P(), P("src"))

    return jax.shard_map(
        local,
        mesh=mesh,
        in_specs=placed,
        out_specs=P(None, "snk", "src", None, "slab", None),
        check_vma=False,
    )
```

time: 186 us -> 71.3 us (0.38)
  waiting for transfers between devices: 85.3 us -> 20.8 us
  other arithmetic: 41.1 us -> 0 us
  Pallas kernels: 0 us -> 30.8 us
  matrix products: 19.4 us -> 0 us
  starting transfers between devices: 0.3 us -> 16.5 us
  local copies, waits for them, and re-layouts: 16.3 us -> 2.9 us
  between operations: 13.3 us -> 0.11 us
  blocking collectives: 10.6 us -> 0 us
    reduce_scatter x2 -> x0, waiting for transfers between devices: 45.8 us -> none  [the longest x1 32.9 us: local(): lax.psum_scatter(slab_part, 'src', scatter_dimension=2, tiled=True)]
    psum x1 -> x0, waiting for transfers between devices: 38.6 us -> none  [local(): picked = lax.psum(term.astype(jnp.bfloat16), 'snk')]
    pallas_call x0 -> x9, Pallas kernels: none -> 30.8 us  [the longest x2 11.6 us: finish(): pl.pallas_call(functools.partial(block_kernel, n), out_shape=shape((nsrc,...]
    ppermute x0 -> x18, waiting for transfers between devices: none -> 20.8 us  [the longest x9 10.2 us: cross(): return lax.ppermute(x, 'src', [(i, i ^ k) for i in range(nsrc)])]
    dot_general x7 -> x0, matrix products: 19.4 us -> none  [the longest x1 10.2 us: local(): jnp.einsum('mtsqrb,smcb->mtsqrc', half, both, preferred_element_type=jnp....]
    ppermute x0 -> x18, starting transfers between devices: none -> 16.5 us  [the longest x9 11.5 us: cross(): return lax.ppermute(x, 'src', [(i, i ^ k) for i in range(nsrc)])]
    add x7 -> x0, other arithmetic: 16.2 us -> none  [the longest x1 15.1 us: local(): dreal = quad[..., :rows, :nev] + quad[..., rows:, nev:]]
    another operation x8 -> x0, other arithmetic: 13.5 us -> none
  transfers between devices with their start and end apart: 4 -> 18, of which waited for: 4 -> 8; matrix products, arithmetic and copies ran while one was open for 5% -> 0% of each run, Pallas kernels for 0% -> 25%
where the time goes in v2:
time: 71.3 us; the launch traced here: 71.2 us
  Pallas kernels  30.8 us (43%)
  waiting for transfers between devices  20.8 us (29%)
  starting transfers between devices  16.5 us (23%)
  local copies, waits for them, and re-layouts  2.9 us (4%)
    pallas_call x2, Pallas kernels, finish(): pl.pallas_call(functools.partial(block_kernel, n), out_shape=shape((nsrc,...  11.6 us
    ppermute x9, starting transfers between devices, cross(): return lax.ppermute(x, 'src', [(i, i ^ k) for i in range(nsrc)])  11.5 us
    ppermute x9, waiting for transfers between devices, cross(): return lax.ppermute(x, 'src', [(i, i ^ k) for i in range(nsrc)])  10.2 us
    ppermute x3, waiting for transfers between devices, along(): return lax.ppermute(x, 'snk', [(i, i ^ d) for i in range(nsnk)])  9.32 us
    pallas_call x1, Pallas kernels, fast(): pl.pallas_call(functools.partial(last_kernel, slabs, lz), out_shape=shape...  5.34 us
    ppermute x3, starting transfers between devices, along(): return lax.ppermute(x, 'snk', [(i, i ^ d) for i in range(nsnk)])  4.45 us
    pallas_call x1, Pallas kernels, fast(): pl.pallas_call(functools.partial(sibling_kernel, slabs, lz, sent), out_sh...  4.1 us
    pallas_call x1, Pallas kernels, fast(): pl.pallas_call(functools.partial(own_kernel, slabs, lz, sent), out_shape=...  4.05 us
  transfers between devices with their start and end apart: 18, of which 8 were waited for; matrix products, arithmetic and copies ran while one was open for 0% of the time, Pallas kernels for 25%

profile of v2, /device:TPU:0, one launch (start us, length us, event | category | flops | bytes accessed | tf_op | source)
XLA Modules:
  0.0 71.2 jit_solution(14516844475069338559)
XLA Ops:
  0.5 1.4 %copy-done.1 = bf16[2,1024,384]{2,1,0:T(8,128)(2,1)S(1)} copy-done((bf16[2,1024,384]{2,1,0:T(8,128)(2,1)S(1)}, bf16[2,1024,384]{2,1,0:T(8,128)(2,1)}, u32[]{:S(2)}) %copy-start.1) | copy-done | bytes 1572888
  2.6 4.1 %gram_own.1.acc_ref = f32[3,192,384]{2,1,0:T(8,128)S(1)} custom-call(s32[4,3]{1,0:T(4,128)S(1)} %copy-done.3, bf16[2,1024,384]{2,1,0:T(8,128)(2,1)S(1)} %copy-done.1), custom_call_target="tpu_custom_call" | custom-call | flops 905969664 | bytes 786432 | tf_op jit(solution)/shard_map/gram_own/pallas_call | solution.py:329
  7.5 4.1 %gram_sibling.1 = (bf16[224,384]{1,0:T(8,128)(2,1)S(1)}, bf16[224,384]{1,0:T(8,128)(2,1)S(1)}, bf16[224,384]{1,0:T(8,128)(2,1)S(1)}) custom-call(s32[4,3]{1,0:T(4,128)S(1)} %copy-done.3, s32[2]{0:T(128)S(1)} %copy-done.4, bf16[2,1024,384]{2,1,0:T(8,128)(2,1)S(1)} %collective-permute-done.eig_ref, f32[3,192,384]{2,1,0:T(8,128)S(1)} %gram_own.1.acc_ref), custom_call_target="tpu_custom_call" | custom-call | flops 905969664 | bytes 786432 | tf_op jit(solution)/shard_map/gram_sibling/pallas_call | solution.py:339
  11.6 2.5 %collective-permute-start.1 = (bf16[224,384]{1,0:T(8,128)(2,1)S(1)}, bf16[224,384]{1,0:T(8,128)(2,1)S(1)}, u32[]{:S(2)}, u32[]{:S(2)}) collective-permute-start(bf16[224,384]{1,0:T(8,128)(2,1)S(1)} %get-tuple-element.14), channel_id=1, source_target_pairs={{0,8},{8,0},{16,24},{24,16},{1,9},{9,1},{17,25},{25,17},{2,10},{10... | collective-permute-start | bytes 516104 | tf_op jit(solution)/shard_map/ppermute | solution.py:308
  14.1 1.5 %collective-permute-start.2 = (bf16[224,384]{1,0:T(8,128)(2,1)S(1)}, bf16[224,384]{1,0:T(8,128)(2,1)S(1)}, u32[]{:S(2)}, u32[]{:S(2)}) collective-permute-start(bf16[224,384]{1,0:T(8,128)(2,1)S(1)} %get-tuple-element.15), channel_id=1, source_target_pairs={{0,16},{8,24},{16,0},{24,8},{1,17},{9,25},{17,1},{25,9},{2,18},{10... | collective-permute-start | bytes 516104 | tf_op jit(solution)/shard_map/ppermute | solution.py:308
  15.7 5.3 %gram_last.1.own = f32[192,384]{1,0:T(8,128)S(1)} custom-call(s32[4,3]{1,0:T(4,128)S(1)} %copy-done.3, bf16[2,1024,384]{2,1,0:T(8,128)(2,1)S(1)} %copy-done.2, bf16[2,1024,384]{2,1,0:T(8,128)(2,1)S(1)} %collective-permute-done.eig_ref), custom_call_target="tpu_custom_call" | custom-call | flops 603979776 | bytes 786432 | tf_op jit(solution)/shard_map/gram_last/pallas_call | solution.py:350
  21.0 3.3 %collective-permute-done.2.refs_1_ = bf16[224,384]{1,0:T(8,128)(2,1)S(1)} collective-permute-done((bf16[224,384]{1,0:T(8,128)(2,1)S(1)}, bf16[224,384]{1,0:T(8,128)(2,1)S(1)}, u32[]{:S(2)}, u32[]{:S(2)}) %collective-permute-start.2) | collective-permute-done | bytes 172064 | tf_op jit(solution)/shard_map/ppermute | solution.py:308
  24.5 1.3 %collective-permute-done.4.came = bf16[96,384]{1,0:T(8,128)(2,1)S(1)} collective-permute-done((bf16[96,384]{1,0:T(8,128)(2,1)S(1)}, bf16[96,384]{1,0:T(8,128)(2,1)S(1)}, u32[]{:S(2)}, u32[]{:S(2)}) %collective-permute-start.4) | collective-permute-done | bytes 73760 | tf_op jit(solution)/shard_map/ppermute | solution.py:305
  25.8 3.7 %collective-permute-start.10 = (bf16[2,96,384]{2,1,0:T(8,128)(2,1)S(1)}, bf16[2,96,384]{2,1,0:T(8,128)(2,1)S(1)}, u32[]{:S(2)}, u32[]{:S(2)}) collective-permute-start(bf16[2,96,384]{2,1,0:T(8,128)(2,1)S(1)} %join.1.refs_0_.refs_3_), channel_id=1, source_target_pairs={{0,6},{2,4},{4,2},{6,0},{1,7},{3,5},{5,3},{7,1},{8,14},{10,12},{12... | collective-permute-start | bytes 442376 | tf_op jit(solution)/shard_map/ppermute | solution.py:311
  30.2 1.5 %collective-permute-start.7 = (bf16[2,96,384]{2,1,0:T(8,128)(2,1)S(1)}, bf16[2,96,384]{2,1,0:T(8,128)(2,1)S(1)}, u32[]{:S(2)}, u32[]{:S(2)}) collective-permute-start(bf16[2,96,384]{2,1,0:T(8,128)(2,1)S(1)} %join.1.refs_0_.refs_3_), channel_id=1, source_target_pairs={{0,24},{8,16},{16,8},{24,0},{1,25},{9,17},{17,9},{25,1},{2,26},{10... | collective-permute-start | bytes 442376 | tf_op jit(solution)/shard_map/ppermute | solution.py:308
  31.7 1.2 %collective-permute-start.6 = (bf16[2,96,384]{2,1,0:T(8,128)(2,1)S(1)}, bf16[2,96,384]{2,1,0:T(8,128)(2,1)S(1)}, u32[]{:S(2)}, u32[]{:S(2)}) collective-permute-start(bf16[2,96,384]{2,1,0:T(8,128)(2,1)S(1)} %join.1.refs_0_.refs_3_), channel_id=1, source_target_pairs={{0,16},{8,24},{16,0},{24,8},{1,17},{9,25},{17,1},{25,9},{2,18},{10... | collective-permute-start | bytes 442376 | tf_op jit(solution)/shard_map/ppermute | solution.py:308
  32.9 1.5 %collective-permute-done.10.refs_6_ = bf16[2,96,384]{2,1,0:T(8,128)(2,1)S(1)} collective-permute-done((bf16[2,96,384]{2,1,0:T(8,128)(2,1)S(1)}, bf16[2,96,384]{2,1,0:T(8,128)(2,1)S(1)}, u32[]{:S(2)}, u32[]{:S(2)}) %collective-permute-start.10) | collective-permute-done | bytes 147488 | tf_op jit(solution)/shard_map/ppermute | solution.py:311
  34.5 7.8 %collective-permute-done.9.refs_5_ = bf16[2,96,384]{2,1,0:T(8,128)(2,1)S(1)} collective-permute-done((bf16[2,96,384]{2,1,0:T(8,128)(2,1)S(1)}, bf16[2,96,384]{2,1,0:T(8,128)(2,1)S(1)}, u32[]{:S(2)}, u32[]{:S(2)}) %collective-permute-start.9) | collective-permute-done | bytes 147488 | tf_op jit(solution)/shard_map/ppermute | solution.py:311
  42.2 1.6 %pick.1 = (bf16[2,96,384]{2,1,0:T(8,128)(2,1)S(1)}, bf16[2,96,384]{2,1,0:T(8,128)(2,1)}, bf16[2,96,384]{2,1,0:T(8,128)(2,1)}, bf16[2,96,384]{2,1,0:T(8,128)(2,1)}) custom-call(s32[2]{0:T(128)S(1)} %copy-done.4, bf16[224,384]{1,0:T(8,128)(2,1)S(1)} %collective-permute-done.1.refs_0_, bf16[224,384]{1,0:T(8,128)(2,1)S(1)} %collective-permute-done.2.refs_1_, ...), custom_call_target="tpu_custom_call" | custom-call | tf_op jit(solution)/shard_map/pick/pallas_call | solution.py:378
  43.9 1.2 %collective-permute-start.11 = (bf16[2,96,384]{2,1,0:T(8,128)(2,1)}, bf16[2,96,384]{2,1,0:T(8,128)(2,1)S(1)}, u32[]{:S(2)}, u32[]{:S(2)}) collective-permute-start(bf16[2,96,384]{2,1,0:T(8,128)(2,1)} %get-tuple-element.19), channel_id=1, source_target_pairs={{0,8},{8,0},{16,24},{24,16},{1,9},{9,1},{17,25},{25,17},{2,10},{10... | collective-permute-start | bytes 442376 | tf_op jit(solution)/shard_map/ppermute | solution.py:308
  45.1 0.8 %collective-permute-start.12 = (bf16[2,96,384]{2,1,0:T(8,128)(2,1)}, bf16[2,96,384]{2,1,0:T(8,128)(2,1)S(1)}, u32[]{:S(2)}, u32[]{:S(2)}) collective-permute-start(bf16[2,96,384]{2,1,0:T(8,128)(2,1)} %get-tuple-element.20), channel_id=1, source_target_pairs={{0,16},{8,24},{16,0},{24,8},{1,17},{9,25},{17,1},{25,9},{2,18},{10... | collective-permute-start | bytes 442376 | tf_op jit(solution)/shard_map/ppermute | solution.py:308
  45.9 1.4 %collective-permute-start.13 = (bf16[2,96,384]{2,1,0:T(8,128)(2,1)}, bf16[2,96,384]{2,1,0:T(8,128)(2,1)S(1)}, u32[]{:S(2)}, u32[]{:S(2)}) collective-permute-start(bf16[2,96,384]{2,1,0:T(8,128)(2,1)} %get-tuple-element.21), channel_id=1, source_target_pairs={{0,24},{8,16},{16,8},{24,0},{1,25},{9,17},{17,9},{25,1},{2,26},{10... | collective-permute-start | bytes 442376 | tf_op jit(solution)/shard_map/ppermute | solution.py:308
  47.4 1.2 %collective-permute-start.5 = (bf16[2,96,384]{2,1,0:T(8,128)(2,1)S(1)}, bf16[2,96,384]{2,1,0:T(8,128)(2,1)S(1)}, u32[]{:S(2)}, u32[]{:S(2)}) collective-permute-start(bf16[2,96,384]{2,1,0:T(8,128)(2,1)S(1)} %join.1.refs_0_.refs_3_), channel_id=1, source_target_pairs={{0,8},{8,0},{16,24},{24,16},{1,9},{9,1},{17,25},{25,17},{2,10},{10... | collective-permute-start | bytes 442376 | tf_op jit(solution)/shard_map/ppermute | solution.py:308
  48.6 1.7 %collective-permute-done.11.refs_0_ = bf16[2,96,384]{2,1,0:T(8,128)(2,1)S(1)} collective-permute-done((bf16[2,96,384]{2,1,0:T(8,128)(2,1)}, bf16[2,96,384]{2,1,0:T(8,128)(2,1)S(1)}, u32[]{:S(2)}, u32[]{:S(2)}) %collective-permute-start.11) | collective-permute-done | bytes 147488 | tf_op jit(solution)/shard_map/ppermute | solution.py:308
  50.3 1.5 %collective-permute-done.12.refs_1_ = bf16[2,96,384]{2,1,0:T(8,128)(2,1)S(1)} collective-permute-done((bf16[2,96,384]{2,1,0:T(8,128)(2,1)}, bf16[2,96,384]{2,1,0:T(8,128)(2,1)S(1)}, u32[]{:S(2)}, u32[]{:S(2)}) %collective-permute-start.12) | collective-permute-done | bytes 147488 | tf_op jit(solution)/shard_map/ppermute | solution.py:308
  51.9 3.0 %collective-permute-done.13.refs_2_ = bf16[2,96,384]{2,1,0:T(8,128)(2,1)S(1)} collective-permute-done((bf16[2,96,384]{2,1,0:T(8,128)(2,1)}, bf16[2,96,384]{2,1,0:T(8,128)(2,1)S(1)}, u32[]{:S(2)}, u32[]{:S(2)}) %collective-permute-start.13) | collective-permute-done | bytes 147488 | tf_op jit(solution)/shard_map/ppermute | solution.py:308
  55.6 4.0 %half.1.half_ref = bf16[4,2,8,96,384]{4,3,2,1,0:T(8,128)(2,1)S(1)} custom-call(bf16[2,96,384]{2,1,0:T(8,128)(2,1)S(1)} %join.1.refs_0_.refs_3_, bf16[2,96,384]{2,1,0:T(8,128)(2,1)S(1)} %collective-permute-done.5.refs_1_, bf16[2,96,384]{2,1,0:T(8,128)(2,1)S(1)} %collective-permute-done.6.refs_2_, bf16[2,96,384]{2,1,0:T(8,128)(2,1)S(1)} %collective-permute-done.7.refs_3_, ...), custom_call_target="tpu_custom_call" | custom-call | flops 1811939328 | bytes 2359296 | tf_op jit(solution)/shard_map/half/pallas_call | solution.py:389
  59.6 3.1 %shard_map.46.refs_6_ = f32[4,2,2,4,96,384]{5,4,3,2,1,0:T(8,128)} custom-call(s32[1]{0:T(128)} %bitcast.index_ref, bf16[4,2,8,96,384]{4,3,2,1,0:T(8,128)(2,1)S(1)} %half.1.half_ref, bf16[2,96,384]{2,1,0:T(8,128)(2,1)S(1)} %get-tuple-element.22.refs_0_, bf16[2,96,384]{2,1,0:T(8,128)(2,1)S(1)} %collective-permute-done.17.refs_1_), custom_call_target="tpu_custom_call" | custom-call | flops 452984832 | bytes 2359296 | tf_op jit(solution)/shard_map/pallas_call | solution.py:411
  62.7 8.5 %shard_map.47 = f32[4,2,2,4,96,384]{5,4,3,2,1,0:T(8,128)} custom-call(s32[1]{0:T(128)} %bitcast.index_ref, bf16[4,2,8,96,384]{4,3,2,1,0:T(8,128)(2,1)S(1)} %half.1.half_ref, bf16[2,96,384]{2,1,0:T(8,128)(2,1)S(1)} %collective-permute-done.11.refs_0_, bf16[2,96,384]{2,1,0:T(8,128)(2,1)S(1)} %collective-permute-done.12.refs_1_, ...), custom_call_target="tpu_custom_call", output_to_operand_aliasing={{}: (8, {})} | custom-call | flops 1358954496 | bytes 7077888 | tf_op jit(solution)/shard_map/pallas_call | solution.py:411
  (31 shorter events, 3.7 us)
Async XLA Ops:
  0.0 6.7 %collective-permute-start = (bf16[2,1024,384]{2,1,0:T(8,128)(2,1)}, bf16[2,1024,384]{2,1,0:T(8,128)(2,1)S(1)}, u32[]{:S(2)}, u32[]{:S(2)}) collective-permute-start(bf16[2,1024,384]{2,1,0:T(8,128)(2,1)} %eig_hbm.3), channel_id=1, source_target_pairs={{0,1},{1,0},{2,3},{3,2},{4,5},{5,4},{6,7},{7,6},{8,9},{9,8},{10,11... | collective-permute-start | bytes 4718600 | tf_op jit(solution)/shard_map/ppermute | solution.py:305
  0.5 1.4 %copy-start.1 = (bf16[2,1024,384]{2,1,0:T(8,128)(2,1)S(1)}, bf16[2,1024,384]{2,1,0:T(8,128)(2,1)}, u32[]{:S(2)}) copy-start(bf16[2,1024,384]{2,1,0:T(8,128)(2,1)} %eig_hbm.3) | copy-start | bytes 4718596
  1.9 0.7 copy-start.3
  2.6 13.1 %copy-start.2 = (bf16[2,1024,384]{2,1,0:T(8,128)(2,1)S(1)}, bf16[2,1024,384]{2,1,0:T(8,128)(2,1)}, u32[]{:S(2)}) copy-start(bf16[2,1024,384]{2,1,0:T(8,128)(2,1)} %eig_hbm.3) | copy-start | bytes 4718596
  6.6 48.9 %copy-start = (bf16[2,2,4,192,384]{4,3,2,1,0:T(8,128)(2,1)S(1)}, bf16[2,2,4,192,384]{4,3,2,1,0:T(8,128)(2,1)}, u32[]{:S(2)}) copy-start(bf16[2,2,4,192,384]{4,3,2,1,0:T(8,128)(2,1)} %refs_4_.1) | copy-start | bytes 7077892
  6.7 0.8 %copy-start.4 = (s32[2]{0:T(128)S(1)}, s32[2]{0:T(128)}, u32[]{:S(2)}) copy-start(s32[2]{0:T(128)} %times_ref.1) | copy-start | bytes 28
  11.6 9.4 %collective-permute-start.1 = (bf16[224,384]{1,0:T(8,128)(2,1)S(1)}, bf16[224,384]{1,0:T(8,128)(2,1)S(1)}, u32[]{:S(2)}, u32[]{:S(2)}) collective-permute-start(bf16[224,384]{1,0:T(8,128)(2,1)S(1)} %get-tuple-element.14), channel_id=1, source_target_pairs={{0,8},{8,0},{16,24},{24,16},{1,9},{9,1},{17,25},{25,17},{2,10},{10... | collective-permute-start | bytes 516104 | tf_op jit(solution)/shard_map/ppermute | solution.py:308
  14.1 10.2 %collective-permute-start.2 = (bf16[224,384]{1,0:T(8,128)(2,1)S(1)}, bf16[224,384]{1,0:T(8,128)(2,1)S(1)}, u32[]{:S(2)}, u32[]{:S(2)}) collective-permute-start(bf16[224,384]{1,0:T(8,128)(2,1)S(1)} %get-tuple-element.15), channel_id=1, source_target_pairs={{0,16},{8,24},{16,0},{24,8},{1,17},{9,25},{17,1},{25,9},{2,18},{10... | collective-permute-start | bytes 516104 | tf_op jit(solution)/shard_map/ppermute | solution.py:308
  15.7 8.7 %collective-permute-start.3 = (bf16[224,384]{1,0:T(8,128)(2,1)S(1)}, bf16[224,384]{1,0:T(8,128)(2,1)S(1)}, u32[]{:S(2)}, u32[]{:S(2)}) collective-permute-start(bf16[224,384]{1,0:T(8,128)(2,1)S(1)} %get-tuple-element.16), channel_id=1, source_target_pairs={{0,24},{8,16},{16,8},{24,0},{1,25},{9,17},{17,9},{25,1},{2,26},{10... | collective-permute-start | bytes 516104 | tf_op jit(solution)/shard_map/ppermute | solution.py:308
  24.4 1.3 %collective-permute-start.4 = (bf16[96,384]{1,0:T(8,128)(2,1)S(1)}, bf16[96,384]{1,0:T(8,128)(2,1)S(1)}, u32[]{:S(2)}, u32[]{:S(2)}) collective-permute-start(bf16[96,384]{1,0:T(8,128)(2,1)S(1)} %get-tuple-element.18), channel_id=1, source_target_pairs={{0,1},{1,0},{2,3},{3,2},{4,5},{5,4},{6,7},{7,6},{8,9},{9,8},{10,11... | collective-permute-start | bytes 221192 | tf_op jit(solution)/shard_map/ppermute | solution.py:305
  25.8 8.7 %collective-permute-start.10 = (bf16[2,96,384]{2,1,0:T(8,128)(2,1)S(1)}, bf16[2,96,384]{2,1,0:T(8,128)(2,1)S(1)}, u32[]{:S(2)}, u32[]{:S(2)}) collective-permute-start(bf16[2,96,384]{2,1,0:T(8,128)(2,1)S(1)} %join.1.refs_0_.refs_3_), channel_id=1, source_target_pairs={{0,6},{2,4},{4,2},{6,0},{1,7},{3,5},{5,3},{7,1},{8,14},{10,12},{12... | collective-permute-start | bytes 442376 | tf_op jit(solution)/shard_map/ppermute | solution.py:311
  29.4 12.8 %collective-permute-start.9 = (bf16[2,96,384]{2,1,0:T(8,128)(2,1)S(1)}, bf16[2,96,384]{2,1,0:T(8,128)(2,1)S(1)}, u32[]{:S(2)}, u32[]{:S(2)}) collective-permute-start(bf16[2,96,384]{2,1,0:T(8,128)(2,1)S(1)} %join.1.refs_0_.refs_3_), channel_id=1, source_target_pairs={{0,4},{2,6},{4,0},{6,2},{1,5},{3,7},{5,1},{7,3},{8,12},{10,14},{12... | collective-permute-start | bytes 442376 | tf_op jit(solution)/shard_map/ppermute | solution.py:311
  29.4 12.8 %collective-permute-start.8 = (bf16[2,96,384]{2,1,0:T(8,128)(2,1)S(1)}, bf16[2,96,384]{2,1,0:T(8,128)(2,1)S(1)}, u32[]{:S(2)}, u32[]{:S(2)}) collective-permute-start(bf16[2,96,384]{2,1,0:T(8,128)(2,1)S(1)} %join.1.refs_0_.refs_3_), channel_id=1, source_target_pairs={{0,2},{2,0},{4,6},{6,4},{1,3},{3,1},{5,7},{7,5},{8,10},{10,8},{12,... | collective-permute-start | bytes 442376 | tf_op jit(solution)/shard_map/ppermute | solution.py:311
  30.2 17.1 %collective-permute-start.7 = (bf16[2,96,384]{2,1,0:T(8,128)(2,1)S(1)}, bf16[2,96,384]{2,1,0:T(8,128)(2,1)S(1)}, u32[]{:S(2)}, u32[]{:S(2)}) collective-permute-start(bf16[2,96,384]{2,1,0:T(8,128)(2,1)S(1)} %join.1.refs_0_.refs_3_), channel_id=1, source_target_pairs={{0,24},{8,16},{16,8},{24,0},{1,25},{9,17},{17,9},{25,1},{2,26},{10... | collective-permute-start | bytes 442376 | tf_op jit(solution)/shard_map/ppermute | solution.py:308
  31.7 16.9 %collective-permute-start.6 = (bf16[2,96,384]{2,1,0:T(8,128)(2,1)S(1)}, bf16[2,96,384]{2,1,0:T(8,128)(2,1)S(1)}, u32[]{:S(2)}, u32[]{:S(2)}) collective-permute-start(bf16[2,96,384]{2,1,0:T(8,128)(2,1)S(1)} %join.1.refs_0_.refs_3_), channel_id=1, source_target_pairs={{0,16},{8,24},{16,0},{24,8},{1,17},{9,25},{17,1},{25,9},{2,18},{10... | collective-permute-start | bytes 442376 | tf_op jit(solution)/shard_map/ppermute | solution.py:308
  43.9 6.5 %collective-permute-start.11 = (bf16[2,96,384]{2,1,0:T(8,128)(2,1)}, bf16[2,96,384]{2,1,0:T(8,128)(2,1)S(1)}, u32[]{:S(2)}, u32[]{:S(2)}) collective-permute-start(bf16[2,96,384]{2,1,0:T(8,128)(2,1)} %get-tuple-element.19), channel_id=1, source_target_pairs={{0,8},{8,0},{16,24},{24,16},{1,9},{9,1},{17,25},{25,17},{2,10},{10... | collective-permute-start | bytes 442376 | tf_op jit(solution)/shard_map/ppermute | solution.py:308
  45.1 6.7 %collective-permute-start.12 = (bf16[2,96,384]{2,1,0:T(8,128)(2,1)}, bf16[2,96,384]{2,1,0:T(8,128)(2,1)S(1)}, u32[]{:S(2)}, u32[]{:S(2)}) collective-permute-start(bf16[2,96,384]{2,1,0:T(8,128)(2,1)} %get-tuple-element.20), channel_id=1, source_target_pairs={{0,16},{8,24},{16,0},{24,8},{1,17},{9,25},{17,1},{25,9},{2,18},{10... | collective-permute-start | bytes 442376 | tf_op jit(solution)/shard_map/ppermute | solution.py:308
  45.9 8.9 %collective-permute-start.13 = (bf16[2,96,384]{2,1,0:T(8,128)(2,1)}, bf16[2,96,384]{2,1,0:T(8,128)(2,1)S(1)}, u32[]{:S(2)}, u32[]{:S(2)}) collective-permute-start(bf16[2,96,384]{2,1,0:T(8,128)(2,1)} %get-tuple-element.21), channel_id=1, source_target_pairs={{0,24},{8,16},{16,8},{24,0},{1,25},{9,17},{17,9},{25,1},{2,26},{10... | collective-permute-start | bytes 442376 | tf_op jit(solution)/shard_map/ppermute | solution.py:308
  47.4 8.2 %collective-permute-start.5 = (bf16[2,96,384]{2,1,0:T(8,128)(2,1)S(1)}, bf16[2,96,384]{2,1,0:T(8,128)(2,1)S(1)}, u32[]{:S(2)}, u32[]{:S(2)}) collective-permute-start(bf16[2,96,384]{2,1,0:T(8,128)(2,1)S(1)} %join.1.refs_0_.refs_3_), channel_id=1, source_target_pairs={{0,8},{8,0},{16,24},{24,16},{1,9},{9,1},{17,25},{25,17},{2,10},{10... | collective-permute-start | bytes 442376 | tf_op jit(solution)/shard_map/ppermute | solution.py:308
  48.6 11.0 %collective-permute-start.17 = (bf16[2,96,384]{2,1,0:T(8,128)(2,1)S(1)}, bf16[2,96,384]{2,1,0:T(8,128)(2,1)S(1)}, u32[]{:S(2)}, u32[]{:S(2)}) collective-permute-start(bf16[2,96,384]{2,1,0:T(8,128)(2,1)S(1)} %get-tuple-element.22.refs_0_), channel_id=1, source_target_pairs={{0,1},{1,0},{2,3},{3,2},{4,5},{5,4},{6,7},{7,6},{8,9},{9,8},{10,11... | collective-permute-start | bytes 442376 | tf_op jit(solution)/shard_map/ppermute | solution.py:305
  50.3 12.3 %collective-permute-start.14 = (bf16[2,96,384]{2,1,0:T(8,128)(2,1)S(1)}, bf16[2,96,384]{2,1,0:T(8,128)(2,1)S(1)}, u32[]{:S(2)}, u32[]{:S(2)}) collective-permute-start(bf16[2,96,384]{2,1,0:T(8,128)(2,1)S(1)} %collective-permute-done.11.refs_0_), channel_id=1, source_target_pairs={{0,1},{1,0},{2,3},{3,2},{4,5},{5,4},{6,7},{7,6},{8,9},{9,8},{10,11... | collective-permute-start | bytes 442376 | tf_op jit(solution)/shard_map/ppermute | solution.py:305
  51.8 10.8 %collective-permute-start.15 = (bf16[2,96,384]{2,1,0:T(8,128)(2,1)S(1)}, bf16[2,96,384]{2,1,0:T(8,128)(2,1)S(1)}, u32[]{:S(2)}, u32[]{:S(2)}) collective-permute-start(bf16[2,96,384]{2,1,0:T(8,128)(2,1)S(1)} %collective-permute-done.12.refs_1_), channel_id=1, source_target_pairs={{0,1},{1,0},{2,3},{3,2},{4,5},{5,4},{6,7},{7,6},{8,9},{9,8},{10,11... | collective-permute-start | bytes 442376 | tf_op jit(solution)/shard_map/ppermute | solution.py:305
  54.8 7.8 %collective-permute-start.16 = (bf16[2,96,384]{2,1,0:T(8,128)(2,1)S(1)}, bf16[2,96,384]{2,1,0:T(8,128)(2,1)S(1)}, u32[]{:S(2)}, u32[]{:S(2)}) collective-permute-start(bf16[2,96,384]{2,1,0:T(8,128)(2,1)S(1)} %collective-permute-done.13.refs_2_), channel_id=1, source_target_pairs={{0,1},{1,0},{2,3},{3,2},{4,5},{5,4},{6,7},{7,6},{8,9},{9,8},{10,11... | collective-permute-start | bytes 442376 | tf_op jit(solution)/shard_map/ppermute | solution.py:305

commit v3 on v2

v3 whole, which is shorter than its diff:
```python
import functools
import math

import jax
import jax.numpy as jnp
from jax import lax
from jax.experimental import pallas as pl
from jax.experimental.pallas import tpu as pltpu
from jax.sharding import PartitionSpec as P


LX = 32
LY = 32
TAIL = 16
CHUNK = 256
F32 = jnp.float32
BF16 = jnp.bfloat16
VMEM = pl.BlockSpec(memory_space=pltpu.VMEM)
SMEM = pl.BlockSpec(memory_space=pltpu.SMEM)


def angles(momenta, xs, ys, zs, lz):
    fx = (momenta[:, 0:1] * xs[None, :] % LX).astype(F32) / LX
    fy = (momenta[:, 1:2] * ys[None, :] % LY).astype(F32) / LY
    fz = (momenta[:, 2:3] * zs[None, :] % lz).astype(F32) / lz
    return 2.0 * math.pi * (fx + fy + fz)


def general(eigvecs, perambulator, momenta, source_times):
    nev = eigvecs.shape[2] // 2
    count = eigvecs.shape[1]
    zpl = count // (LX * LY)
    slabs = lax.axis_size("slab")
    lz = zpl * lax.axis_size("src") * slabs
    sites = jnp.arange(count, dtype=jnp.int32)
    xs = sites % LX
    ys = sites // LX % LY
    zs = sites // (LX * LY) + lax.axis_index(("src", "slab")) * zpl
    angle = angles(momenta, xs, ys, zs, lz)
    vreal = eigvecs[:, :, :nev].astype(F32)
    vimag = eigvecs[:, :, nev:].astype(F32)
    partials = []
    for m in range(angle.shape[0]):
        cosine = jnp.cos(angle[m])[None, :, None]
        sine = jnp.sin(angle[m])[None, :, None]
        phased = jnp.concatenate(
            [cosine * vreal + sine * vimag, cosine * vimag - sine * vreal], axis=2
        ).astype(BF16)
        gram = jnp.einsum("tsa,tsb->tab", eigvecs, phased, preferred_element_type=F32)
        real = gram[:, :nev, :nev] + gram[:, nev:, nev:]
        imag = gram[:, :nev, nev:] - gram[:, nev:, :nev]
        partials.append(jnp.concatenate([real, imag], axis=2))
    partial_value = jnp.stack(partials, axis=1)
    tdev = partial_value.shape[0]
    rows = nev // slabs
    local_times = lax.axis_index("snk") * tdev + jnp.arange(tdev, dtype=jnp.int32)
    slab_part = lax.psum_scatter(partial_value, "slab", scatter_dimension=2, tiled=True)
    share = lax.psum_scatter(slab_part, "src", scatter_dimension=2, tiled=True).astype(BF16)
    sink = lax.all_gather(share, "src", axis=2, tiled=True)
    selector = (source_times[:, None] == local_times[None, :]).astype(BF16)
    term = jnp.dot(selector, sink.reshape(tdev, -1), preferred_element_type=F32)
    picked = lax.psum(term.astype(BF16), "snk")
    picked = picked.reshape((source_times.shape[0],) + sink.shape[1:])
    source = lax.all_gather(picked, "slab", axis=2, tiled=True)
    stacked = jnp.concatenate([sink[..., :nev], sink[..., nev:]], axis=2)
    prod = jnp.einsum("tmra,tsqab->mtsqrb", stacked, perambulator, preferred_element_type=F32)
    creal = prod[..., :rows, :nev] - prod[..., rows:, nev:]
    cimag = prod[..., :rows, nev:] + prod[..., rows:, :nev]
    half = jnp.concatenate([creal, cimag], axis=4).astype(BF16)
    both = jnp.concatenate([source[..., :nev], source[..., nev:]], axis=2)
    quad = jnp.einsum("mtsqrb,smcb->mtsqrc", half, both, preferred_element_type=F32)
    dreal = quad[..., :rows, :nev] + quad[..., rows:, nev:]
    dimag = quad[..., rows:, :nev] - quad[..., :rows, nev:]
    return jnp.concatenate([dreal, dimag], axis=-1)


def turned(x, nev):
    return jnp.concatenate([x[:, nev:], -x[:, :nev]], axis=1)


def circle(f):
    turns = jnp.floor(4.0 * f + 0.5)
    r = (f - 0.25 * turns) * (2.0 * math.pi)
    n = turns.astype(jnp.int32) & 3
    x = r * r
    c = 1.0 + x * (-1 / 2 + x * (1 / 24 + x * (-1 / 720 + x * (1 / 40320))))
    s = r * (1.0 + x * (-1 / 6 + x * (1 / 120 + x * (-1 / 5040 + x * (1 / 362880)))))
    odd = (n & 1) == 1
    cosine = jnp.where(odd, s, c)
    sine = jnp.where(odd, c, s)
    return (
        jnp.where((n == 1) | (n == 2), -cosine, cosine),
        jnp.where(n >= 2, -sine, sine),
    )


def phase(tab, i, y, core, width):
    cy = jnp.broadcast_to(tab[2 + 2 * core, i, pl.ds(y, 1), :], (LX, 128))
    sy = jnp.broadcast_to(tab[3 + 2 * core, i, pl.ds(y, 1), :], (LX, 128))
    cx, sx = tab[0, i], tab[1, i]
    c = cx * cy - sx * sy
    s = sx * cy + cx * sy
    return [jnp.concatenate([x] * (width // 128), axis=1) for x in (c, s)]


def site_sums(pieces, vec, tab, core, wide, tran, sums):
    count, width = vec.shape
    nev = width // 2
    chunk = min(count, CHUNK)

    def spread(c):
        for y in range(c * chunk // LX, (c + 1) * chunk // LX):
            at = pl.ds(y * LX, LX)
            v = vec[at, :].astype(F32)
            u = turned(v, nev)
            for i, k in enumerate(pieces):
                c_, s_ = phase(tab, k, y, core, width)
                wide[at, i * width : (i + 1) * width] = (c_ * v + s_ * u).astype(BF16)

    tran[...] = vec[...].T
    spread(0)
    for c in range(count // chunk):
        at = slice(c * chunk, (c + 1) * chunk)
        for i in range(len(pieces)):
            g = jnp.dot(
                tran[:, at], wide[at, i * width : (i + 1) * width], preferred_element_type=F32
            )
            sums[i] = g if c == 0 else sums[i] + g
        if (c + 1) * chunk < count:
            spread(c + 1)


def own_kernel(nsrc, slabs, lz, pieces, mom_hbm, eig_hbm, acc_ref, tab, vec, *refs):
    mom_ref, wide, tran, sums, mom_sem, sem = refs
    nev = vec.shape[1] // 2
    slab = lax.axis_index("slab")
    src = lax.axis_index("src")
    small = pltpu.make_async_copy(mom_hbm, mom_ref, mom_sem)
    small.start()
    copy = pltpu.make_async_copy(eig_hbm.at[slab], vec, sem)
    copy.start()
    small.wait()
    index = lax.broadcasted_iota(jnp.int32, (LX, 128), 0)
    for k in range(nsrc):
        mom = mom_ref[pl.ds(src ^ k, 1), :]
        px, py, pz = (jnp.broadcast_to(mom[:, i : i + 1], (LX, 128)) for i in range(3))
        tab[0, k], tab[1, k] = circle((px * index % LX).astype(F32) / LX)
        for core in range(2):
            z = src * slabs + (1 - slab if core else slab)
            fz = (pz * z % lz).astype(F32) / lz
            fy = (py * index % LY).astype(F32) / LY
            tab[2 + 2 * core, k], tab[3 + 2 * core, k] = circle(fy + fz)
    copy.wait()
    site_sums(pieces, vec, tab, 0, wide, tran, sums)
    for i in range(len(pieces)):
        acc_ref[i] = sums[i, :nev] + turned(sums[i, nev:], nev)


def sibling_kernel(pieces, times_hbm, eig_ref, tab, acc_ref, *refs):
    outs = refs[: len(pieces)]
    times_ref, wide, tran, sums, sem = refs[len(pieces) :]
    copy = pltpu.make_async_copy(times_hbm, times_ref, sem)
    copy.start()
    width = eig_ref.shape[2]
    nev = width // 2
    site_sums(pieces, eig_ref.at[lax.axis_index("slab")], tab, 1, wide, tran, sums)
    copy.wait()
    for i in range(len(pieces)):
        e = sums[i, :nev] + turned(sums[i, nev:], nev)
        outs[i][:nev, :] = (e + acc_ref[i]).astype(BF16)
        for s in range(times_ref.shape[1]):
            time = jnp.broadcast_to(times_ref[:, s : s + 1].astype(F32), (TAIL, width))
            outs[i][nev + s * TAIL : nev + (s + 1) * TAIL, :] = time.astype(BF16)


def last_kernel(eig_hbm, eig_ref, tab, out, vec, wide, tran, sums, sem):
    nev = vec.shape[1] // 2
    slab = lax.axis_index("slab")
    copy = pltpu.make_async_copy(eig_hbm.at[slab], vec, sem)
    copy.start()
    site_sums([0], eig_ref.at[slab], tab, 1, wide, tran, sums)
    out[...] = sums[0, :nev] + turned(sums[0, nev:], nev)
    copy.wait()
    site_sums([0], vec, tab, 0, wide, tran, sums)
    out[...] = out[...] + (sums[0, :nev] + turned(sums[0, nev:], nev))


def sum_kernel(own, *refs):
    keep, send = refs[-2:]
    rows = keep.shape[0]
    slab = lax.axis_index("slab")
    for out, part in ((keep, slab), (send, 1 - slab)):
        at = pl.multiple_of(part * rows, rows)
        total = own[pl.ds(at, rows), :]
        for r in refs[:-2]:
            total = total + r[pl.ds(at, rows), :].astype(F32)
        out[...] = total.astype(BF16)


def join_kernel(keep, came, out):
    slab = lax.axis_index("slab")
    out[slab] = keep[...]
    out[1 - slab] = came[...]


def pick_kernel(nsnk, nsrc, times_ref, *refs):
    sent = refs[: nsrc - 1]
    seen = refs[nsrc - 1 : nsrc - 1 + nsnk]
    outs = refs[nsrc - 1 + nsnk :]
    tdev, rows, width = seen[0].shape
    nev = width // 2
    snk = lax.axis_index("snk")
    for k in range(nsrc):
        for s in range(outs[k].shape[0]):
            if k == 0:
                want = jnp.full((TAIL, 128), times_ref[s].astype(F32), F32)
            else:
                want = sent[k - 1][nev + s * TAIL : nev + (s + 1) * TAIL, :128].astype(F32)
            mask = []
            for d in range(nsnk):
                for t in range(tdev):
                    time = ((snk ^ d) * tdev + t).astype(F32)
                    one = (want == time).astype(F32).astype(BF16)
                    mask.append(jnp.concatenate([one] * (width // 128), axis=1))
            for r in range(rows // TAIL):
                total = None
                for d in range(nsnk):
                    for t in range(tdev):
                        term = mask[d * tdev + t] * seen[d][t, r * TAIL : (r + 1) * TAIL, :]
                        total = term if total is None else total + term
                outs[k][s, r * TAIL : (r + 1) * TAIL, :] = total


def half_kernel(nsrc, *refs):
    sinks = refs[:nsrc]
    per_ref, out_ref, lhs, rhs = refs[nsrc:]
    tdev, rows, width = sinks[0].shape
    nev = width // 2
    sdev, nq = per_ref.shape[1:3]
    for t in range(tdev):
        for k in range(nsrc):
            lhs[t, k * rows : (k + 1) * rows, :] = sinks[k][t]
        for s in range(sdev):
            for q in range(nq):
                p = per_ref[t, s, q]
                rhs[s, :nev, q * width : (q + 1) * width] = p
                rhs[s, nev:, q * width : (q + 1) * width] = (-turned(p.astype(F32), nev)).astype(BF16)
            h = jnp.dot(lhs[t], rhs[s], preferred_element_type=F32).astype(BF16)
            for q in range(nq):
                for k in range(nsrc):
                    part = h[k * rows : (k + 1) * rows, q * width : (q + 1) * width]
                    out_ref[k, s, t * nq + q] = part


def block_kernel(first, pieces, chained, half_ref, *refs):
    mine = refs[:pieces]
    other = refs[pieces : 2 * pieces]
    out_hbm, rhs, buf, sem = refs[2 * pieces + chained :]
    sdev, rows, width = mine[0].shape
    nev = width // 2
    slots, tdev, nq = buf.shape[:3]
    slab = lax.axis_index("slab")
    src = lax.axis_index("src")
    copies = []
    for j in range(pieces):
        for s in range(sdev):
            n = len(copies)
            slot, part = n % slots, n % 2
            lower = jnp.where(slab == 0, mine[j][s], other[j][s])
            upper = jnp.where(slab == 0, other[j][s], mine[j][s])
            for at, x in ((0, lower), (rows, upper)):
                rhs[part, at : at + rows, :] = x
                rhs[part, nev + at : nev + at + rows, :] = (-turned(x.astype(F32), nev)).astype(BF16)
            if n >= slots:
                for copy in copies[n - slots]:
                    copy.wait()
            out = lax.dot_general(
                half_ref[first + j, s].reshape(tdev * nq * rows, width),
                rhs[part],
                (((1,), (1,)), ((), ())),
                preferred_element_type=F32,
            )
            buf[slot] = out.reshape(tdev, nq, rows, width)
            copies.append(
                [
                    pltpu.make_async_copy(
                        buf.at[slot, t], out_hbm.at[src ^ (first + j), t, s], sem.at[slot, t]
                    )
                    for t in range(tdev)
                ]
            )
            for copy in copies[n]:
                copy.start()
    for group in copies[-slots:]:
        for copy in group:
            copy.wait()


def fast(eigvecs, perambulator, momenta, source_times):
    nsrc, nsnk, slabs = (lax.axis_size(a) for a in ("src", "snk", "slab"))
    tdev, count, width = eigvecs.shape
    sdev = source_times.shape[0]
    nq = perambulator.shape[2]
    nev = width // 2
    rows = nev // slabs
    lz = count // (LX * LY) * nsrc * slabs

    def shape(dims, dtype=BF16):
        return jax.ShapeDtypeStruct(dims, dtype)

    def params(mib):
        return pltpu.CompilerParams(vmem_limit_bytes=mib * 2**20)

    def cost(flops, moved):
        return pl.CostEstimate(flops=flops, bytes_accessed=moved, transcendentals=0)

    def swap(x):
        return lax.ppermute(x, "slab", [(0, 1), (1, 0)])

    def cross(x, k):
        return lax.ppermute(x, "src", [(i, i ^ k) for i in range(nsrc)])

    def along(x, d):
        return lax.ppermute(x, "snk", [(i, i ^ d) for i in range(nsnk)])

    theirs = swap(eigvecs)
    work = 2 * width * count * width
    hbm = pl.BlockSpec(memory_space=pltpu.HBM)
    sent = list(range(nsrc - 1, 0, -1))

    def grams(n):
        return [
            pltpu.VMEM((count, n * width), BF16),
            pltpu.VMEM((width, count), BF16),
            pltpu.VMEM((n, width, width), F32),
        ]

    vec = pltpu.VMEM((count, width), BF16)
    sem = pltpu.SemaphoreType.DMA

    def held(x):
        return pltpu.with_memory_space_constraint(x, pltpu.HBM)

    eigs = held(eigvecs)
    acc, tab = pl.pallas_call(
        functools.partial(own_kernel, nsrc, slabs, lz, sent),
        out_shape=[shape((len(sent), nev, width), F32), shape((6, nsrc, LX, 128), F32)],
        in_specs=[hbm, hbm],
        out_specs=[VMEM] * 2,
        scratch_shapes=[vec, pltpu.VMEM(momenta.shape, jnp.int32)] + grams(len(sent)) + [sem] * 2,
        cost_estimate=cost(len(sent) * work, 2 * count * width),
        compiler_params=params(12),
        name="gram_own",
    )(held(momenta), eigs)
    parts = pl.pallas_call(
        functools.partial(sibling_kernel, sent),
        out_shape=[shape((nev + sdev * TAIL, width))] * len(sent),
        in_specs=[hbm] + [VMEM] * 3,
        out_specs=[VMEM] * len(sent),
        scratch_shapes=[pltpu.VMEM((1, sdev), jnp.int32)] + grams(len(sent)) + [sem],
        cost_estimate=cost(len(sent) * work, 2 * count * width),
        compiler_params=params(12),
        name="gram_sibling",
    )(held(source_times.reshape(1, sdev)), theirs, tab, acc)
    got = [cross(part, k) for k, part in zip(sent, parts)][::-1]
    own = pl.pallas_call(
        last_kernel,
        out_shape=shape((nev, width), F32),
        in_specs=[hbm, VMEM, VMEM],
        out_specs=VMEM,
        scratch_shapes=[vec] + grams(1) + [sem],
        cost_estimate=cost(2 * work, 2 * count * width),
        compiler_params=params(12),
        name="gram_last",
    )(eigs, theirs, tab)
    keep, send = pl.pallas_call(
        sum_kernel,
        out_shape=[shape((rows, width))] * 2,
        in_specs=[VMEM] * nsrc,
        out_specs=[VMEM] * 2,
        compiler_params=params(4),
        name="sum",
    )(own, *got)
    red = pl.pallas_call(
        join_kernel,
        out_shape=shape((tdev, rows, width)),
        in_specs=[VMEM] * 2,
        out_specs=VMEM,
        compiler_params=params(4),
        name="join",
    )(keep, swap(send))
    seen = [red] + [along(red, d) for d in range(1, nsnk)]
    sinks = [red] + [cross(red, k) for k in range(1, nsrc)]
    picked = pl.pallas_call(
        functools.partial(pick_kernel, nsnk, nsrc),
        out_shape=[shape((sdev, rows, width))] * nsrc,
        in_specs=[SMEM] + [VMEM] * (nsrc - 1 + nsnk),
        out_specs=[VMEM] * nsrc,
        compiler_params=params(8),
        name="pick",
    )(source_times, *got, *seen)

    tq = tdev * nq
    half = pl.pallas_call(
        functools.partial(half_kernel, nsrc),
        out_shape=shape((nsrc, sdev, tq, rows, width)),
        in_specs=[VMEM] * (nsrc + 1),
        out_specs=VMEM,
        scratch_shapes=[
            pltpu.VMEM((tdev, nsrc * rows, width), BF16),
            pltpu.VMEM((sdev, width, nq * width), BF16),
        ],
        cost_estimate=cost(2 * tq * sdev * nsrc * rows * width * width, 2 * perambulator.size),
        compiler_params=params(16),
        name="half",
    )(*sinks, perambulator)

    mine = [picked[0]] + [cross(picked[k], k) for k in range(1, nsrc)]
    other = [swap(x) for x in mine]

    def finish(first, n, before):
        chained = before is not None
        slots = min(n * sdev, 4)
        return pl.pallas_call(
            functools.partial(block_kernel, first, n, chained),
            out_shape=shape((nsrc, tdev, sdev, nq, rows, width), F32),
            in_specs=[VMEM] * (1 + 2 * n) + [hbm] * chained,
            out_specs=hbm,
            scratch_shapes=[
                pltpu.VMEM((2, width, width), BF16),
                pltpu.VMEM((slots, tdev, nq, rows, width), F32),
                pltpu.SemaphoreType.DMA((slots, tdev)),
            ],
            input_output_aliases={1 + 2 * n: 0} if chained else {},
            cost_estimate=cost(
                2 * n * tq * sdev * rows * width * width, 4 * n * tq * sdev * rows * width
            ),
            compiler_params=params(16),
        )(half, *mine[first : first + n], *other[first : first + n], *([before] if chained else []))

    blocks = finish(0, 1, None)
    return finish(1, nsrc - 1, blocks)


def local(eigvecs, perambulator, momenta, source_times):
    nsrc = lax.axis_size("src")
    fits = (
        lax.axis_size("slab") == 2
        and momenta.shape[0] == nsrc
        and nsrc & (nsrc - 1) == 0
        and eigvecs.shape[1] == LX * LY
        and source_times.shape[0] == eigvecs.shape[0]
    )
    return (fast if fits else general)(eigvecs, perambulator, momenta, source_times)


def solution(mesh):
    placed = (P("snk", ("src", "slab"), None), P("snk", "src", None, None, None), P(), P("src"))

    return jax.shard_map(
        local,
        mesh=mesh,
        in_specs=placed,
        out_specs=P(None, "snk", "src", None, "slab", None),
        check_vma=False,
    )
```

time: 71.3 us -> 59 us (0.83)
  Pallas kernels: 30.8 us -> 18.5 us
  local copies, waits for them, and re-layouts: 2.9 us -> 0.01 us
  waiting for transfers between devices: 20.8 us -> 23.4 us
    pallas_call x5, Pallas kernels: 25.1 us -> 14.7 us  [the longest x2 6.07 us: finish(): pl.pallas_call(functools.partial(block_kernel, first, n, chained), out_sh...]
    unnamed x10 -> x4, local copies, waits for them, and re-layouts: 2.9 us -> 0.01 us
    ppermute x9, waiting for transfers between devices: 10.2 us -> 12.8 us  [cross(): return lax.ppermute(x, 'src', [(i, i ^ k) for i in range(nsrc)])]
    pallas_call x1, Pallas kernels: 3.99 us -> 2.73 us  [fast(): pl.pallas_call(functools.partial(half_kernel, nsrc), out_shape=shape((nsr...]
  transfers between devices with their start and end apart: 18 -> 18, of which waited for: 8 -> 9; matrix products, arithmetic and copies ran while one was open for 0% -> 0% of each run, Pallas kernels for 25% -> 20%
where the time goes in v3:
time: 59 us; the launch traced here: 58.9 us
  waiting for transfers between devices  23.4 us (40%)
  Pallas kernels  18.5 us (31%)
  starting transfers between devices  16.7 us (28%)
    ppermute x9, waiting for transfers between devices, cross(): return lax.ppermute(x, 'src', [(i, i ^ k) for i in range(nsrc)])  12.8 us
    ppermute x9, starting transfers between devices, cross(): return lax.ppermute(x, 'src', [(i, i ^ k) for i in range(nsrc)])  11.7 us
    ppermute x3, waiting for transfers between devices, along(): return lax.ppermute(x, 'snk', [(i, i ^ d) for i in range(nsnk)])  9.32 us
    pallas_call x2, Pallas kernels, finish(): pl.pallas_call(functools.partial(block_kernel, first, n, chained), out_sh...  6.07 us
    ppermute x3, starting transfers between devices, along(): return lax.ppermute(x, 'snk', [(i, i ^ d) for i in range(nsnk)])  4.45 us
    pallas_call x1, Pallas kernels, fast(): pl.pallas_call(functools.partial(own_kernel, nsrc, slabs, lz, sent), out_...  3.41 us
    pallas_call x1, Pallas kernels, fast(): pl.pallas_call(functools.partial(sibling_kernel, sent), out_shape=[shape(...  2.74 us
    pallas_call x1, Pallas kernels, fast(): pl.pallas_call(functools.partial(half_kernel, nsrc), out_shape=shape((nsr...  2.73 us
  transfers between devices with their start and end apart: 18, of which 9 were waited for; matrix products, arithmetic and copies ran while one was open for 0% of the time, Pallas kernels for 20%

profile of v3, /device:TPU:0, one launch (start us, length us, event | category | flops | bytes accessed | tf_op | source)
XLA Modules:
  0.0 58.9 jit_solution(17234391322453565604)
XLA Ops:
  0.5 3.4 %gram_own.1 = (f32[3,192,384]{2,1,0:T(8,128)S(1)}, f32[6,4,32,128]{3,2,1,0:T(8,128)S(1)}) custom-call(s32[4,3]{1,0:T(4,128)} %mom_hbm.1, bf16[2,1024,384]{2,1,0:T(8,128)(2,1)} %eig_hbm.3), custom_call_target="tpu_custom_call" | custom-call | flops 905969664 | bytes 786432 | tf_op jit(solution)/shard_map/gram_own/pallas_call | solution.py:345
  4.0 2.7 %gram_sibling.1 = (bf16[224,384]{1,0:T(8,128)(2,1)S(1)}, bf16[224,384]{1,0:T(8,128)(2,1)S(1)}, bf16[224,384]{1,0:T(8,128)(2,1)S(1)}) custom-call(s32[1,2]{1,0:T(1,128)} %bitcast.1, bf16[2,1024,384]{2,1,0:T(8,128)(2,1)S(1)} %collective-permute-done.eig_ref, f32[6,4,32,128]{3,2,1,0:T(8,128)S(1)} %get-tuple-element.16.tab, ...), custom_call_target="tpu_custom_call" | custom-call | flops 905969664 | bytes 786432 | tf_op jit(solution)/shard_map/gram_sibling/pallas_call | solution.py:355
  6.7 2.7 %collective-permute-start.1 = (bf16[224,384]{1,0:T(8,128)(2,1)S(1)}, bf16[224,384]{1,0:T(8,128)(2,1)S(1)}, u32[]{:S(2)}, u32[]{:S(2)}) collective-permute-start(bf16[224,384]{1,0:T(8,128)(2,1)S(1)} %get-tuple-element.18), channel_id=1, source_target_pairs={{0,8},{8,0},{16,24},{24,16},{1,9},{9,1},{17,25},{25,17},{2,10},{10... | collective-permute-start | bytes 516104 | tf_op jit(solution)/shard_map/ppermute | solution.py:321
  9.4 1.5 %collective-permute-start.2 = (bf16[224,384]{1,0:T(8,128)(2,1)S(1)}, bf16[224,384]{1,0:T(8,128)(2,1)S(1)}, u32[]{:S(2)}, u32[]{:S(2)}) collective-permute-start(bf16[224,384]{1,0:T(8,128)(2,1)S(1)} %get-tuple-element.19), channel_id=1, source_target_pairs={{0,16},{8,24},{16,0},{24,8},{1,17},{9,25},{17,1},{25,9},{2,18},{10... | collective-permute-start | bytes 516104 | tf_op jit(solution)/shard_map/ppermute | solution.py:321
  10.9 2.4 %gram_last.1.own = f32[192,384]{1,0:T(8,128)S(1)} custom-call(bf16[2,1024,384]{2,1,0:T(8,128)(2,1)} %eig_hbm.3, bf16[2,1024,384]{2,1,0:T(8,128)(2,1)S(1)} %collective-permute-done.eig_ref, f32[6,4,32,128]{3,2,1,0:T(8,128)S(1)} %get-tuple-element.16.tab), custom_call_target="tpu_custom_call" | custom-call | flops 603979776 | bytes 786432 | tf_op jit(solution)/shard_map/gram_last/pallas_call | solution.py:366
  13.4 1.2 %collective-permute-done.1.refs_0_ = bf16[224,384]{1,0:T(8,128)(2,1)S(1)} collective-permute-done((bf16[224,384]{1,0:T(8,128)(2,1)S(1)}, bf16[224,384]{1,0:T(8,128)(2,1)S(1)}, u32[]{:S(2)}, u32[]{:S(2)}) %collective-permute-start.1) | collective-permute-done | bytes 172064 | tf_op jit(solution)/shard_map/ppermute | solution.py:321
  14.6 4.8 %collective-permute-done.2.refs_1_ = bf16[224,384]{1,0:T(8,128)(2,1)S(1)} collective-permute-done((bf16[224,384]{1,0:T(8,128)(2,1)S(1)}, bf16[224,384]{1,0:T(8,128)(2,1)S(1)}, u32[]{:S(2)}, u32[]{:S(2)}) %collective-permute-start.2) | collective-permute-done | bytes 172064 | tf_op jit(solution)/shard_map/ppermute | solution.py:321
  19.6 1.3 %collective-permute-done.4.came = bf16[96,384]{1,0:T(8,128)(2,1)S(1)} collective-permute-done((bf16[96,384]{1,0:T(8,128)(2,1)S(1)}, bf16[96,384]{1,0:T(8,128)(2,1)S(1)}, u32[]{:S(2)}, u32[]{:S(2)}) %collective-permute-start.4) | collective-permute-done | bytes 73760 | tf_op jit(solution)/shard_map/ppermute | solution.py:318
  20.9 3.7 %collective-permute-start.10 = (bf16[2,96,384]{2,1,0:T(8,128)(2,1)S(1)}, bf16[2,96,384]{2,1,0:T(8,128)(2,1)S(1)}, u32[]{:S(2)}, u32[]{:S(2)}) collective-permute-start(bf16[2,96,384]{2,1,0:T(8,128)(2,1)S(1)} %join.1.refs_0_.refs_3_), channel_id=1, source_target_pairs={{0,6},{2,4},{4,2},{6,0},{1,7},{3,5},{5,3},{7,1},{8,14},{10,12},{12... | collective-permute-start | bytes 442376 | tf_op jit(solution)/shard_map/ppermute | solution.py:324
  25.3 1.5 %collective-permute-start.7 = (bf16[2,96,384]{2,1,0:T(8,128)(2,1)S(1)}, bf16[2,96,384]{2,1,0:T(8,128)(2,1)S(1)}, u32[]{:S(2)}, u32[]{:S(2)}) collective-permute-start(bf16[2,96,384]{2,1,0:T(8,128)(2,1)S(1)} %join.1.refs_0_.refs_3_), channel_id=1, source_target_pairs={{0,24},{8,16},{16,8},{24,0},{1,25},{9,17},{17,9},{25,1},{2,26},{10... | collective-permute-start | bytes 442376 | tf_op jit(solution)/shard_map/ppermute | solution.py:321
  26.8 1.2 %collective-permute-start.6 = (bf16[2,96,384]{2,1,0:T(8,128)(2,1)S(1)}, bf16[2,96,384]{2,1,0:T(8,128)(2,1)S(1)}, u32[]{:S(2)}, u32[]{:S(2)}) collective-permute-start(bf16[2,96,384]{2,1,0:T(8,128)(2,1)S(1)} %join.1.refs_0_.refs_3_), channel_id=1, source_target_pairs={{0,16},{8,24},{16,0},{24,8},{1,17},{9,25},{17,1},{25,9},{2,18},{10... | collective-permute-start | bytes 442376 | tf_op jit(solution)/shard_map/ppermute | solution.py:321
  28.0 1.5 %collective-permute-done.10.refs_6_ = bf16[2,96,384]{2,1,0:T(8,128)(2,1)S(1)} collective-permute-done((bf16[2,96,384]{2,1,0:T(8,128)(2,1)S(1)}, bf16[2,96,384]{2,1,0:T(8,128)(2,1)S(1)}, u32[]{:S(2)}, u32[]{:S(2)}) %collective-permute-start.10) | collective-permute-done | bytes 147488 | tf_op jit(solution)/shard_map/ppermute | solution.py:324
  29.6 7.8 %collective-permute-done.9.refs_5_ = bf16[2,96,384]{2,1,0:T(8,128)(2,1)S(1)} collective-permute-done((bf16[2,96,384]{2,1,0:T(8,128)(2,1)S(1)}, bf16[2,96,384]{2,1,0:T(8,128)(2,1)S(1)}, u32[]{:S(2)}, u32[]{:S(2)}) %collective-permute-start.9) | collective-permute-done | bytes 147488 | tf_op jit(solution)/shard_map/ppermute | solution.py:324
  37.4 1.0 %pick.1 = (bf16[2,96,384]{2,1,0:T(8,128)(2,1)S(1)}, bf16[2,96,384]{2,1,0:T(8,128)(2,1)S(1)}, bf16[2,96,384]{2,1,0:T(8,128)(2,1)S(1)}, bf16[2,96,384]{2,1,0:T(8,128)(2,1)S(1)}) custom-call(s32[2]{0:T(128)S(1)} %copy-done.1, bf16[224,384]{1,0:T(8,128)(2,1)S(1)} %collective-permute-done.1.refs_0_, bf16[224,384]{1,0:T(8,128)(2,1)S(1)} %collective-permute-done.2.refs_1_, ...), custom_call_target="tpu_custom_call" | custom-call | tf_op jit(solution)/shard_map/pick/pallas_call | solution.py:394
  38.3 1.3 %collective-permute-start.11 = (bf16[2,96,384]{2,1,0:T(8,128)(2,1)S(1)}, bf16[2,96,384]{2,1,0:T(8,128)(2,1)S(1)}, u32[]{:S(2)}, u32[]{:S(2)}) collective-permute-start(bf16[2,96,384]{2,1,0:T(8,128)(2,1)S(1)} %get-tuple-element.23), channel_id=1, source_target_pairs={{0,8},{8,0},{16,24},{24,16},{1,9},{9,1},{17,25},{25,17},{2,10},{10... | collective-permute-start | bytes 442376 | tf_op jit(solution)/shard_map/ppermute | solution.py:321
  39.6 0.8 %collective-permute-start.12 = (bf16[2,96,384]{2,1,0:T(8,128)(2,1)S(1)}, bf16[2,96,384]{2,1,0:T(8,128)(2,1)S(1)}, u32[]{:S(2)}, u32[]{:S(2)}) collective-permute-start(bf16[2,96,384]{2,1,0:T(8,128)(2,1)S(1)} %get-tuple-element.24), channel_id=1, source_target_pairs={{0,16},{8,24},{16,0},{24,8},{1,17},{9,25},{17,1},{25,9},{2,18},{10... | collective-permute-start | bytes 442376 | tf_op jit(solution)/shard_map/ppermute | solution.py:321
  40.4 1.4 %collective-permute-start.13 = (bf16[2,96,384]{2,1,0:T(8,128)(2,1)S(1)}, bf16[2,96,384]{2,1,0:T(8,128)(2,1)S(1)}, u32[]{:S(2)}, u32[]{:S(2)}) collective-permute-start(bf16[2,96,384]{2,1,0:T(8,128)(2,1)S(1)} %get-tuple-element.25), channel_id=1, source_target_pairs={{0,24},{8,16},{16,8},{24,0},{1,25},{9,17},{17,9},{25,1},{2,26},{10... | collective-permute-start | bytes 442376 | tf_op jit(solution)/shard_map/ppermute | solution.py:321
  41.9 1.2 %collective-permute-start.5 = (bf16[2,96,384]{2,1,0:T(8,128)(2,1)S(1)}, bf16[2,96,384]{2,1,0:T(8,128)(2,1)S(1)}, u32[]{:S(2)}, u32[]{:S(2)}) collective-permute-start(bf16[2,96,384]{2,1,0:T(8,128)(2,1)S(1)} %join.1.refs_0_.refs_3_), channel_id=1, source_target_pairs={{0,8},{8,0},{16,24},{24,16},{1,9},{9,1},{17,25},{25,17},{2,10},{10... | collective-permute-start | bytes 442376 | tf_op jit(solution)/shard_map/ppermute | solution.py:321
  43.1 1.5 %collective-permute-done.11.refs_0_ = bf16[2,96,384]{2,1,0:T(8,128)(2,1)S(1)} collective-permute-done((bf16[2,96,384]{2,1,0:T(8,128)(2,1)S(1)}, bf16[2,96,384]{2,1,0:T(8,128)(2,1)S(1)}, u32[]{:S(2)}, u32[]{:S(2)}) %collective-permute-start.11) | collective-permute-done | bytes 147488 | tf_op jit(solution)/shard_map/ppermute | solution.py:321
  44.6 1.5 %collective-permute-done.12.refs_1_ = bf16[2,96,384]{2,1,0:T(8,128)(2,1)S(1)} collective-permute-done((bf16[2,96,384]{2,1,0:T(8,128)(2,1)S(1)}, bf16[2,96,384]{2,1,0:T(8,128)(2,1)S(1)}, u32[]{:S(2)}, u32[]{:S(2)}) %collective-permute-start.12) | collective-permute-done | bytes 147488 | tf_op jit(solution)/shard_map/ppermute | solution.py:321
  46.1 3.0 %collective-permute-done.13.refs_2_ = bf16[2,96,384]{2,1,0:T(8,128)(2,1)S(1)} collective-permute-done((bf16[2,96,384]{2,1,0:T(8,128)(2,1)S(1)}, bf16[2,96,384]{2,1,0:T(8,128)(2,1)S(1)}, u32[]{:S(2)}, u32[]{:S(2)}) %collective-permute-start.13) | collective-permute-done | bytes 147488 | tf_op jit(solution)/shard_map/ppermute | solution.py:321
  49.8 2.7 %half.1.half_ref = bf16[4,2,8,96,384]{4,3,2,1,0:T(8,128)(2,1)S(1)} custom-call(bf16[2,96,384]{2,1,0:T(8,128)(2,1)S(1)} %join.1.refs_0_.refs_3_, bf16[2,96,384]{2,1,0:T(8,128)(2,1)S(1)} %collective-permute-done.5.refs_1_, bf16[2,96,384]{2,1,0:T(8,128)(2,1)S(1)} %collective-permute-done.6.refs_2_, bf16[2,96,384]{2,1,0:T(8,128)(2,1)S(1)} %collective-permute-done.7.refs_3_, ...), custom_call_target="tpu_custom_call" | custom-call | flops 1811939328 | bytes 2359296 | tf_op jit(solution)/shard_map/half/pallas_call | solution.py:404
  52.6 2.1 %shard_map.46.refs_6_ = f32[4,2,2,4,96,384]{5,4,3,2,1,0:T(8,128)} custom-call(bf16[4,2,8,96,384]{4,3,2,1,0:T(8,128)(2,1)S(1)} %half.1.half_ref, bf16[2,96,384]{2,1,0:T(8,128)(2,1)S(1)} %get-tuple-element.26.refs_0_, bf16[2,96,384]{2,1,0:T(8,128)(2,1)S(1)} %collective-permute-done.17.refs_1_), custom_call_target="tpu_custom_call" | custom-call | flops 452984832 | bytes 2359296 | tf_op jit(solution)/shard_map/pallas_call | solution.py:424
  54.7 4.0 %shard_map.47 = f32[4,2,2,4,96,384]{5,4,3,2,1,0:T(8,128)} custom-call(bf16[4,2,8,96,384]{4,3,2,1,0:T(8,128)(2,1)S(1)} %half.1.half_ref, bf16[2,96,384]{2,1,0:T(8,128)(2,1)S(1)} %collective-permute-done.11.refs_0_, bf16[2,96,384]{2,1,0:T(8,128)(2,1)S(1)} %collective-permute-done.12.refs_1_, ...), custom_call_target="tpu_custom_call", output_to_operand_aliasing={{}: (7, {})} | custom-call | flops 1358954496 | bytes 7077888 | tf_op jit(solution)/shard_map/pallas_call | solution.py:424
  (25 shorter events, 2.2 us)
Async XLA Ops:
  0.0 3.9 %collective-permute-start = (bf16[2,1024,384]{2,1,0:T(8,128)(2,1)}, bf16[2,1024,384]{2,1,0:T(8,128)(2,1)S(1)}, u32[]{:S(2)}, u32[]{:S(2)}) collective-permute-start(bf16[2,1024,384]{2,1,0:T(8,128)(2,1)} %eig_hbm.3), channel_id=1, source_target_pairs={{0,1},{1,0},{2,3},{3,2},{4,5},{5,4},{6,7},{7,6},{8,9},{9,8},{10,11... | collective-permute-start | bytes 4718600 | tf_op jit(solution)/shard_map/ppermute | solution.py:318
  3.9 33.4 %copy-start.1 = (s32[2]{0:T(128)S(1)}, s32[2]{0:T(128)}, u32[]{:S(2)}) copy-start(s32[2]{0:T(128)} %times_ref.1) | copy-start | bytes 28
  3.9 45.9 %copy-start = (bf16[2,2,4,192,384]{4,3,2,1,0:T(8,128)(2,1)S(1)}, bf16[2,2,4,192,384]{4,3,2,1,0:T(8,128)(2,1)}, u32[]{:S(2)}) copy-start(bf16[2,2,4,192,384]{4,3,2,1,0:T(8,128)(2,1)} %refs_4_.1) | copy-start | bytes 7077892
  6.7 7.9 %collective-permute-start.1 = (bf16[224,384]{1,0:T(8,128)(2,1)S(1)}, bf16[224,384]{1,0:T(8,128)(2,1)S(1)}, u32[]{:S(2)}, u32[]{:S(2)}) collective-permute-start(bf16[224,384]{1,0:T(8,128)(2,1)S(1)} %get-tuple-element.18), channel_id=1, source_target_pairs={{0,8},{8,0},{16,24},{24,16},{1,9},{9,1},{17,25},{25,17},{2,10},{10... | collective-permute-start | bytes 516104 | tf_op jit(solution)/shard_map/ppermute | solution.py:321
  9.4 10.0 %collective-permute-start.2 = (bf16[224,384]{1,0:T(8,128)(2,1)S(1)}, bf16[224,384]{1,0:T(8,128)(2,1)S(1)}, u32[]{:S(2)}, u32[]{:S(2)}) collective-permute-start(bf16[224,384]{1,0:T(8,128)(2,1)S(1)} %get-tuple-element.19), channel_id=1, source_target_pairs={{0,16},{8,24},{16,0},{24,8},{1,17},{9,25},{17,1},{25,9},{2,18},{10... | collective-permute-start | bytes 516104 | tf_op jit(solution)/shard_map/ppermute | solution.py:321
  10.9 8.5 %collective-permute-start.3 = (bf16[224,384]{1,0:T(8,128)(2,1)S(1)}, bf16[224,384]{1,0:T(8,128)(2,1)S(1)}, u32[]{:S(2)}, u32[]{:S(2)}) collective-permute-start(bf16[224,384]{1,0:T(8,128)(2,1)S(1)} %get-tuple-element.20), channel_id=1, source_target_pairs={{0,24},{8,16},{16,8},{24,0},{1,25},{9,17},{17,9},{25,1},{2,26},{10... | collective-permute-start | bytes 516104 | tf_op jit(solution)/shard_map/ppermute | solution.py:321
  19.5 1.3 %collective-permute-start.4 = (bf16[96,384]{1,0:T(8,128)(2,1)S(1)}, bf16[96,384]{1,0:T(8,128)(2,1)S(1)}, u32[]{:S(2)}, u32[]{:S(2)}) collective-permute-start(bf16[96,384]{1,0:T(8,128)(2,1)S(1)} %get-tuple-element.22), channel_id=1, source_target_pairs={{0,1},{1,0},{2,3},{3,2},{4,5},{5,4},{6,7},{7,6},{8,9},{9,8},{10,11... | collective-permute-start | bytes 221192 | tf_op jit(solution)/shard_map/ppermute | solution.py:318
  20.9 8.7 %collective-permute-start.10 = (bf16[2,96,384]{2,1,0:T(8,128)(2,1)S(1)}, bf16[2,96,384]{2,1,0:T(8,128)(2,1)S(1)}, u32[]{:S(2)}, u32[]{:S(2)}) collective-permute-start(bf16[2,96,384]{2,1,0:T(8,128)(2,1)S(1)} %join.1.refs_0_.refs_3_), channel_id=1, source_target_pairs={{0,6},{2,4},{4,2},{6,0},{1,7},{3,5},{5,3},{7,1},{8,14},{10,12},{12... | collective-permute-start | bytes 442376 | tf_op jit(solution)/shard_map/ppermute | solution.py:324
  24.6 12.8 %collective-permute-start.9 = (bf16[2,96,384]{2,1,0:T(8,128)(2,1)S(1)}, bf16[2,96,384]{2,1,0:T(8,128)(2,1)S(1)}, u32[]{:S(2)}, u32[]{:S(2)}) collective-permute-start(bf16[2,96,384]{2,1,0:T(8,128)(2,1)S(1)} %join.1.refs_0_.refs_3_), channel_id=1, source_target_pairs={{0,4},{2,6},{4,0},{6,2},{1,5},{3,7},{5,1},{7,3},{8,12},{10,14},{12... | collective-permute-start | bytes 442376 | tf_op jit(solution)/shard_map/ppermute | solution.py:324
  24.6 12.8 %collective-permute-start.8 = (bf16[2,96,384]{2,1,0:T(8,128)(2,1)S(1)}, bf16[2,96,384]{2,1,0:T(8,128)(2,1)S(1)}, u32[]{:S(2)}, u32[]{:S(2)}) collective-permute-start(bf16[2,96,384]{2,1,0:T(8,128)(2,1)S(1)} %join.1.refs_0_.refs_3_), channel_id=1, source_target_pairs={{0,2},{2,0},{4,6},{6,4},{1,3},{3,1},{5,7},{7,5},{8,10},{10,8},{12,... | collective-permute-start | bytes 442376 | tf_op jit(solution)/shard_map/ppermute | solution.py:324
  25.3 16.5 %collective-permute-start.7 = (bf16[2,96,384]{2,1,0:T(8,128)(2,1)S(1)}, bf16[2,96,384]{2,1,0:T(8,128)(2,1)S(1)}, u32[]{:S(2)}, u32[]{:S(2)}) collective-permute-start(bf16[2,96,384]{2,1,0:T(8,128)(2,1)S(1)} %join.1.refs_0_.refs_3_), channel_id=1, source_target_pairs={{0,24},{8,16},{16,8},{24,0},{1,25},{9,17},{17,9},{25,1},{2,26},{10... | collective-permute-start | bytes 442376 | tf_op jit(solution)/shard_map/ppermute | solution.py:321
  26.8 16.3 %collective-permute-start.6 = (bf16[2,96,384]{2,1,0:T(8,128)(2,1)S(1)}, bf16[2,96,384]{2,1,0:T(8,128)(2,1)S(1)}, u32[]{:S(2)}, u32[]{:S(2)}) collective-permute-start(bf16[2,96,384]{2,1,0:T(8,128)(2,1)S(1)} %join.1.refs_0_.refs_3_), channel_id=1, source_target_pairs={{0,16},{8,24},{16,0},{24,8},{1,17},{9,25},{17,1},{25,9},{2,18},{10... | collective-permute-start | bytes 442376 | tf_op jit(solution)/shard_map/ppermute | solution.py:321
  38.3 6.3 %collective-permute-start.11 = (bf16[2,96,384]{2,1,0:T(8,128)(2,1)S(1)}, bf16[2,96,384]{2,1,0:T(8,128)(2,1)S(1)}, u32[]{:S(2)}, u32[]{:S(2)}) collective-permute-start(bf16[2,96,384]{2,1,0:T(8,128)(2,1)S(1)} %get-tuple-element.23), channel_id=1, source_target_pairs={{0,8},{8,0},{16,24},{24,16},{1,9},{9,1},{17,25},{25,17},{2,10},{10... | collective-permute-start | bytes 442376 | tf_op jit(solution)/shard_map/ppermute | solution.py:321
  39.6 6.5 %collective-permute-start.12 = (bf16[2,96,384]{2,1,0:T(8,128)(2,1)S(1)}, bf16[2,96,384]{2,1,0:T(8,128)(2,1)S(1)}, u32[]{:S(2)}, u32[]{:S(2)}) collective-permute-start(bf16[2,96,384]{2,1,0:T(8,128)(2,1)S(1)} %get-tuple-element.24), channel_id=1, source_target_pairs={{0,16},{8,24},{16,0},{24,8},{1,17},{9,25},{17,1},{25,9},{2,18},{10... | collective-permute-start | bytes 442376 | tf_op jit(solution)/shard_map/ppermute | solution.py:321
  40.4 8.7 %collective-permute-start.13 = (bf16[2,96,384]{2,1,0:T(8,128)(2,1)S(1)}, bf16[2,96,384]{2,1,0:T(8,128)(2,1)S(1)}, u32[]{:S(2)}, u32[]{:S(2)}) collective-permute-start(bf16[2,96,384]{2,1,0:T(8,128)(2,1)S(1)} %get-tuple-element.25), channel_id=1, source_target_pairs={{0,24},{8,16},{16,8},{24,0},{1,25},{9,17},{17,9},{25,1},{2,26},{10... | collective-permute-start | bytes 442376 | tf_op jit(solution)/shard_map/ppermute | solution.py:321
  41.9 8.0 %collective-permute-start.5 = (bf16[2,96,384]{2,1,0:T(8,128)(2,1)S(1)}, bf16[2,96,384]{2,1,0:T(8,128)(2,1)S(1)}, u32[]{:S(2)}, u32[]{:S(2)}) collective-permute-start(bf16[2,96,384]{2,1,0:T(8,128)(2,1)S(1)} %join.1.refs_0_.refs_3_), channel_id=1, source_target_pairs={{0,8},{8,0},{16,24},{24,16},{1,9},{9,1},{17,25},{25,17},{2,10},{10... | collective-permute-start | bytes 442376 | tf_op jit(solution)/shard_map/ppermute | solution.py:321
  43.1 9.5 %collective-permute-start.17 = (bf16[2,96,384]{2,1,0:T(8,128)(2,1)S(1)}, bf16[2,96,384]{2,1,0:T(8,128)(2,1)S(1)}, u32[]{:S(2)}, u32[]{:S(2)}) collective-permute-start(bf16[2,96,384]{2,1,0:T(8,128)(2,1)S(1)} %get-tuple-element.26.refs_0_), channel_id=1, source_target_pairs={{0,1},{1,0},{2,3},{3,2},{4,5},{5,4},{6,7},{7,6},{8,9},{9,8},{10,11... | collective-permute-start | bytes 442376 | tf_op jit(solution)/shard_map/ppermute | solution.py:318
  44.6 10.1 %collective-permute-start.14 = (bf16[2,96,384]{2,1,0:T(8,128)(2,1)S(1)}, bf16[2,96,384]{2,1,0:T(8,128)(2,1)S(1)}, u32[]{:S(2)}, u32[]{:S(2)}) collective-permute-start(bf16[2,96,384]{2,1,0:T(8,128)(2,1)S(1)} %collective-permute-done.11.refs_0_), channel_id=1, source_target_pairs={{0,1},{1,0},{2,3},{3,2},{4,5},{5,4},{6,7},{7,6},{8,9},{9,8},{10,11... | collective-permute-start | bytes 442376 | tf_op jit(solution)/shard_map/ppermute | solution.py:318
  46.1 8.6 %collective-permute-start.15 = (bf16[2,96,384]{2,1,0:T(8,128)(2,1)S(1)}, bf16[2,96,384]{2,1,0:T(8,128)(2,1)S(1)}, u32[]{:S(2)}, u32[]{:S(2)}) collective-permute-start(bf16[2,96,384]{2,1,0:T(8,128)(2,1)S(1)} %collective-permute-done.12.refs_1_), channel_id=1, source_target_pairs={{0,1},{1,0},{2,3},{3,2},{4,5},{5,4},{6,7},{7,6},{8,9},{9,8},{10,11... | collective-permute-start | bytes 442376 | tf_op jit(solution)/shard_map/ppermute | solution.py:318
  49.1 5.6 %collective-permute-start.16 = (bf16[2,96,384]{2,1,0:T(8,128)(2,1)S(1)}, bf16[2,96,384]{2,1,0:T(8,128)(2,1)S(1)}, u32[]{:S(2)}, u32[]{:S(2)}) collective-permute-start(bf16[2,96,384]{2,1,0:T(8,128)(2,1)S(1)} %collective-permute-done.13.refs_2_), channel_id=1, source_target_pairs={{0,1},{1,0},{2,3},{3,2},{4,5},{5,4},{6,7},{7,6},{8,9},{9,8},{10,11... | collective-permute-start | bytes 442376 | tf_op jit(solution)/shard_map/ppermute | solution.py:318
